TPU v7x, 32 devices: a whole 2x2x4 slice. The times are simulated.
32 devices in a mesh: shard: 4 (over z), tensor: 4 (over x, core), dp: 2 (over y).
Axes of the slice: x: 2, y: 2, z: 4, core: 2. Of those that a mesh axis runs over, the one named last changes fastest.
Arguments:
- gradient: bfloat16 [1, 8192, 8192], P(None, 'shard', ('tensor', 'dp')), may hold values from -16 to 16
- momentum: float32 [1, 8192, 8192], P(None, 'shard', ('tensor', 'dp')), may hold values from -16 to 16
- prior_right_factor: float32 [1, 8192, 128], P(None, ('tensor', 'dp')), may hold values from -8 to 8
Outputs:
- momentum_next: float32 [1, 8192, 8192], P(None, 'shard', ('tensor', 'dp'))
- following_right_factor: float32 [1, 8192, 128], P(None, ('tensor', 'dp'))
- direction: bfloat16 [1, 8192, 8192], P(None, 'shard', ('tensor', 'dp'))
All inputs are finite; a program needn't handle non-finite values.
Results may differ from a plain program's by a relative error of at most 0.0029.
Values sent between devices are 32-bit elements; how exact they have to be, the bound alone decides.
A program may use at most 64 MiB of HBM per device.

v0:
```python
import functools

import jax
import jax.numpy as jnp
from jax import lax
from jax.experimental import pallas as pl
from jax.experimental.pallas import tpu as pltpu
from jax.sharding import PartitionSpec as P

MESH = pl.DeviceIdType.MESH
HIGHEST = lax.Precision.HIGHEST
decay_rate = 0.95
epsilon = 1e-06
CHUNKS = 8
STEPS = 4


def dot(a, b, dims, precision=HIGHEST):
    return lax.dot_general(
        a, b, (dims, ((), ())), precision=precision, preferred_element_type=jnp.float32
    )


def split(value):
    high = value.astype(jnp.bfloat16)
    low = (value - high.astype(jnp.float32)).astype(jnp.bfloat16)
    return high, low


def product(lhs, rhs):
    high, low = split(lhs)
    pair = jnp.concatenate(split(rhs), axis=1)
    both = dot(high, pair, ((1,), (0,)), None) + dot(low, pair, ((1,), (0,)), None)
    width = rhs.shape[1]
    return both[:, :width] + both[:, width:]


def inverse_factor(gram):
    size = gram.shape[0]
    sub = lax.broadcasted_iota(jnp.int32, (8, size), 0)
    lane = lax.broadcasted_iota(jnp.int32, (8, size), 1)
    rows = lax.broadcasted_iota(jnp.int32, (size, size), 0)
    lanes = lax.broadcasted_iota(jnp.int32, (size, size), 1)

    def row(value, index):
        return jnp.broadcast_to(value[index : index + 1], value.shape)

    def block(step, a):
        top = a[:8]
        columns = [jnp.broadcast_to(top[:, c : c + 1], (8, size)) for c in range(8)]
        panel = jnp.where(lane < 8, jnp.where(lane == sub, 1.0, 0.0), top)
        scale = jnp.zeros((8, size), jnp.float32)
        for c in range(8):
            inverse_root = lax.rsqrt(row(columns[c], c))
            scale = jnp.where(sub == c, inverse_root, scale)
            factor = jnp.where(sub > c, columns[c] * (inverse_root * inverse_root), 0.0)
            panel = panel - factor * row(panel, c)
            for j in range(c + 1, 8):
                columns[j] = columns[j] - factor * row(columns[j], c)
        square = scale * scale
        solved = panel * square
        for c in range(7, 0, -1):
            solved = solved - jnp.where(sub < c, columns[c] * square, 0.0) * row(solved, c)
        active = rows < size - 8 * step
        source = jnp.where(active, a, 0.0)[8:]
        rest = jnp.where(active & (lanes < 8), 0.0, a)[8:]
        for c in range(8):
            rest = rest - jnp.broadcast_to(source[:, c : c + 1], rest.shape) * jnp.broadcast_to(
                solved[c : c + 1], rest.shape
            )
        return pltpu.roll(jnp.concatenate([rest, panel * scale], axis=0), size - 8, 1)

    return jnp.where(rows >= lanes, lax.fori_loop(0, size // 8, block, gram), 0.0)


class Group:
    def __init__(self, count, me, where):
        self.count, self.me, self.where = count, me, where

    def peer(self, k):
        other = lax.rem(self.me + k, self.count)
        return other, self.where(other)


def groups(shape):
    s, t, d = lax.axis_index("shard"), lax.axis_index("tensor"), lax.axis_index("dp")
    tensor, dp = shape["tensor"], shape["dp"]
    cores = 2 if tensor % 2 == 0 else 1
    core, x = lax.rem(t, cores), lax.div(t, cores)
    return {
        "core": Group(cores, core, lambda j: {"tensor": x * cores + j}),
        "x": Group(tensor // cores, x, lambda j: {"tensor": j * cores + core}),
        "y": Group(dp, d, lambda j: {"dp": j}),
        "z": Group(shape["shard"], s, lambda j: {"shard": j}),
        "plane": Group(
            tensor * dp, t * dp + d, lambda j: {"tensor": lax.div(j, dp), "dp": lax.rem(j, dp)}
        ),
    }


def stage_plan(shape, rows):
    cores = 2 if shape["tensor"] % 2 == 0 else 1
    sizes = {"core": cores, "x": shape["tensor"] // cores, "y": shape["dp"]}
    members = shape["tensor"] * shape["dp"]
    halves = 2 if rows % (16 * members) == 0 else 1
    orders = (("core", "x", "y"), ("core", "y", "x"))[:halves]
    return sizes, halves, orders


def factors(shape, momentum_ref, gradient_ref, prior_ref, basis_ref, right_ref, following_ref, *scratch):
    (mixed, raw, left, whole, local, pieces, piece_in, piece_z, piece_all, shares, share_in, squares, load_sem,
     gram_send, gram_recv, share_send,
     share_recv, full_send, full_recv, square_send, square_recv, prior_vmem,
     prior_sem, *stages) = scratch
    rows, cols = mixed.shape
    rank = prior_ref.shape[1]
    where = groups(shape)
    sizes, halves, orders = stage_plan(shape, rows)
    part = rows // CHUNKS

    def load(i):
        at = pl.ds(pl.multiple_of(i * part, 8), part)
        return (
            pltpu.make_async_copy(momentum_ref.at[at], mixed.at[at], load_sem.at[0, i]),
            pltpu.make_async_copy(gradient_ref.at[at], raw.at[at], load_sem.at[1, i]),
        )

    prior_copy = pltpu.make_async_copy(prior_ref, prior_vmem, prior_sem)
    prior_copy.start()
    for i in range(CHUNKS):
        for copy in load(i):
            copy.start()

    barrier = pltpu.get_barrier_semaphore()
    peers = 0
    for name in ("plane", "z"):
        for k in range(1, where[name].count):
            pl.semaphore_signal(barrier, inc=1, device_id=where[name].peer(k)[1], device_id_type=MESH)
            peers += 1
    pl.semaphore_wait(barrier, peers)

    plane, z = where["plane"], where["z"]
    piece = rank // plane.count

    def summed(slots, count):
        total = slots[0]
        for i in range(1, count):
            total = total + slots[i]
        return total

    def sends(group, turn, stage, source, target):
        copies = []
        for k in range(1, group.count):
            other, device = group.peer(k)
            copy = pltpu.make_async_remote_copy(
                src_ref=source(other),
                dst_ref=target,
                send_sem=gram_send.at[turn, stage, k - 1],
                recv_sem=gram_recv.at[turn, stage, k - 1],
                device_id=device,
                device_id_type=MESH,
            )
            copy.start()
            copies.append(copy)
        return copies

    def gram_steps(turn, values):
        gram = sum(dot(value, value, ((0,), (0,))) for value in values)
        for i in range(plane.count):
            pieces[turn, i] = gram[i * piece : (i + 1) * piece]
        piece_in[turn, plane.me] = pieces[turn, plane.me]
        copies = sends(plane, turn, 0, lambda i: pieces.at[turn, i], piece_in.at[turn, plane.me])
        yield
        for copy in copies:
            copy.wait()
        piece_z[turn, z.me] = summed(piece_in.at[turn], plane.count)
        own = piece_z.at[turn, z.me]
        copies = sends(z, turn, 1, lambda i: own, own)
        yield
        for copy in copies:
            copy.wait()
        piece_all[turn, plane.me] = summed(piece_z.at[turn], z.count)
        own = piece_all.at[turn, plane.me]
        copies = sends(plane, turn, 2, lambda i: own, own)
        yield
        for copy in copies:
            copy.wait()
        yield jnp.concatenate([piece_all[turn, i] for i in range(plane.count)], axis=0)

    prior_copy.wait()
    prior = prior_vmem[...]

    def first(i, carry):
        for copy in load(i):
            copy.wait()
        at = pl.ds(pl.multiple_of(i * part, 8), part)
        value = mixed[at, :] + raw[at, :].astype(jnp.float32)
        mixed[at, :] = value
        left[at, :] = product(value, prior)
        return carry

    lax.fori_loop(0, CHUNKS, first, 0)

    starts = [h * (rows // halves) for h in range(halves)]
    sizes_now = [rows // halves] * halves
    trail = []
    for level in range(3):
        pending = []
        for h in range(halves):
            name = orders[h][level]
            group = where[name]
            buffer, send_sem, recv_sem = stages[level * 6 + h * 3 : level * 6 + h * 3 + 3] if halves == 2 else stages[level * 3 : level * 3 + 3]
            if group.count == 1:
                continue
            size = sizes_now[h] // group.count
            copies = []
            for k in range(1, group.count):
                other, device = group.peer(k)
                copy = pltpu.make_async_remote_copy(
                    src_ref=left.at[pl.ds(pl.multiple_of(starts[h] + other * size, 8), size)],
                    dst_ref=buffer.at[k - 1],
                    send_sem=send_sem.at[k - 1],
                    recv_sem=recv_sem.at[k - 1],
                    device_id=device,
                    device_id_type=MESH,
                )
                copy.start()
                copies.append(copy)
            pending.append((h, group, size, copies, buffer))
        for h, group, size, copies, buffer in pending:
            for copy in copies:
                copy.wait()
            own = pl.multiple_of(starts[h] + group.me * size, 8)
            total = left[pl.ds(own, size), :]
            for k in range(group.count - 1):
                total = total + buffer[k]
            left[pl.ds(own, size), :] = total
            starts[h], sizes_now[h] = own, size
            trail.append((level, h, group, own, size))
    for h in range(halves):
        own = pl.ds(starts[h], sizes_now[h])
        whole[own, :] = left[own, :]
    for level in (2, 1, 0):
        copies = []
        for stage, h, group, own, size in trail:
            if stage != level:
                continue
            index = (level * 2 + h) if halves == 2 else level
            for k in range(1, group.count):
                other, device = group.peer(k)
                at = pl.ds(own, size)
                copy = pltpu.make_async_remote_copy(
                    src_ref=whole.at[at],
                    dst_ref=whole.at[at],
                    send_sem=full_send.at[index, k - 1],
                    recv_sem=full_recv.at[index, k - 1],
                    device_id=device,
                    device_id_type=MESH,
                )
                copy.start()
                copies.append(copy)
        if level == 2:
            steps = gram_steps(0, [left[pl.ds(starts[h], sizes_now[h]), :] for h in range(halves)])
            next(steps)
        elif level == 1:
            next(steps)
        else:
            next(steps)
            inverse = inverse_factor(next(steps))
            owned = [
                dot(left[pl.ds(starts[h], sizes_now[h]), :], inverse, ((1,), (1,))) for h in range(halves)
            ]
            steps = gram_steps(1, owned)
            next(steps)
        for copy in copies:
            copy.wait()

    def exchange(slots, group, send_sem, recv_sem):
        copies = []
        for k in range(1, group.count):
            copy = pltpu.make_async_remote_copy(
                src_ref=slots.at[group.me],
                dst_ref=slots.at[group.me],
                send_sem=send_sem.at[k - 1],
                recv_sem=recv_sem.at[k - 1],
                device_id=group.peer(k)[1],
                device_id_type=MESH,
            )
            copy.start()
            copies.append(copy)
        return copies

    value = dot(whole[...], inverse, ((1,), (1,)))
    basis_ref[...] = value
    next(steps)
    high, low = split(value)
    half = cols // 2
    for c in range(2):
        wide_high, wide_low = split(mixed[:, c * half : (c + 1) * half])
        both = dot(jnp.concatenate([high, low], axis=1), wide_high, ((0,), (0,)), None)
        local[:, c * half : (c + 1) * half] = (
            both[:rank] + both[rank:] + dot(high, wide_low, ((0,), (0,)), None)
        )
        if c == 0:
            next(steps)
    share = rank // z.count
    share_copies = []
    for k in range(1, z.count):
        other, device = z.peer(k)
        copy = pltpu.make_async_remote_copy(
            src_ref=local.at[pl.ds(pl.multiple_of(other * share, 8), share)],
            dst_ref=share_in.at[k - 1],
            send_sem=share_send.at[k - 1],
            recv_sem=share_recv.at[k - 1],
            device_id=device,
            device_id_type=MESH,
        )
        copy.start()
        share_copies.append(copy)
    inverse = inverse_factor(next(steps))
    for copy in share_copies:
        copy.wait()
    total = local[pl.ds(pl.multiple_of(z.me * share, 8), share), :]
    for k in range(z.count - 1):
        total = total + share_in[k]
    shares[z.me] = total
    full = exchange(shares, z, full_send.at[full_send.shape[0] - 1], full_recv.at[full_recv.shape[0] - 1])
    basis_ref[...] = dot(basis_ref[...], inverse, ((1,), (1,)))
    for copy in full:
        copy.wait()
    stacked = jnp.concatenate([shares[i] for i in range(z.count)], axis=0)
    right = dot(stacked, inverse, ((0,), (1,)))
    right_ref[...] = right
    squares[plane.me] = jnp.broadcast_to(jnp.sum(right * right, axis=0, keepdims=True), (8, rank))
    for copy in exchange(squares, plane, square_send, square_recv):
        copy.wait()
    mean = summed(squares, plane.count)[:1] / (cols * plane.count)
    following_ref[...] = right / jnp.sqrt(mean + epsilon)


def finish(scale, momentum_ref, gradient_ref, basis_ref, right_ref, following_ref, next_ref, direction_ref):
    high, low = split(basis_ref[...])
    right = right_ref[...].astype(jnp.bfloat16)
    follow_high, follow_low = split(following_ref[...])
    dims = ((1,), (1,))
    next_ref[...] = (
        momentum_ref[...]
        + gradient_ref[...].astype(jnp.float32)
        - (1.0 - decay_rate) * dot(high, right, dims, None)
    )
    product = dot(
        jnp.concatenate([high, low], axis=1), jnp.concatenate([follow_high, follow_high], axis=1), dims, None
    ) + dot(high, follow_low, dims, None)
    direction_ref[...] = (scale * product).astype(jnp.bfloat16)


def shards(shape, gradient, momentum, prior_right_factor):
    gradient, momentum, prior = gradient[0], momentum[0], prior_right_factor[0]
    rows, cols = momentum.shape
    rank = prior.shape[1]
    sizes, halves, orders = stage_plan(shape, rows)
    stages = []
    now = [rows // halves] * halves
    widest = max(max(sizes.values()), shape["shard"], 2) - 1
    for level in range(3):
        for h in range(halves):
            count = sizes[orders[h][level]]
            now[h] //= count
            stages += [
                pltpu.VMEM((max(count - 1, 1), now[h], rank), jnp.float32),
                pltpu.SemaphoreType.DMA((max(count - 1, 1),)),
                pltpu.SemaphoreType.DMA((max(count - 1, 1),)),
            ]
    z = shape["shard"]
    plane = shape["tensor"] * shape["dp"]
    dma = pltpu.SemaphoreType.DMA
    vmem = pl.BlockSpec(memory_space=pltpu.VMEM)
    anywhere = pl.BlockSpec(memory_space=pl.ANY)
    f32 = jnp.float32
    basis, right, following = pl.pallas_call(
        functools.partial(factors, shape),
        out_shape=[
            jax.ShapeDtypeStruct((rows, rank), f32),
            jax.ShapeDtypeStruct((cols, rank), f32),
            jax.ShapeDtypeStruct((cols, rank), f32),
        ],
        in_specs=[anywhere, anywhere, anywhere],
        out_specs=[vmem, vmem, vmem],
        scratch_shapes=[
            pltpu.VMEM((rows, cols), f32),
            pltpu.VMEM((rows, cols), jnp.bfloat16),
            pltpu.VMEM((rows, rank), f32),
            pltpu.VMEM((rows, rank), f32),
            pltpu.VMEM((rank, cols), f32),
            pltpu.VMEM((2, plane, rank // plane, rank), f32),
            pltpu.VMEM((2, plane, rank // plane, rank), f32),
            pltpu.VMEM((2, z, rank // plane, rank), f32),
            pltpu.VMEM((2, plane, rank // plane, rank), f32),
            pltpu.VMEM((z, rank // z, cols), f32),
            pltpu.VMEM((max(z - 1, 1), rank // z, cols), f32),
            pltpu.VMEM((plane, 8, rank), f32),
            dma((2, CHUNKS)),
            dma((2, 3, max(plane, z))),
            dma((2, 3, max(plane, z))),
            dma((max(z - 1, 1),)),
            dma((max(z - 1, 1),)),
            dma((3 * halves + 1, widest)),
            dma((3 * halves + 1, widest)),
            dma((max(plane - 1, 1),)),
            dma((max(plane - 1, 1),)),
            pltpu.VMEM((cols, rank), f32),
            dma,
            *stages,
        ],
        compiler_params=pltpu.CompilerParams(
            collective_id=0, has_side_effects=True, vmem_limit_bytes=48 * 1024 * 1024
        ),
        name="factors",
    )(momentum, gradient, prior)

    block = rows // STEPS
    wide = pl.BlockSpec((block, cols), lambda i: (i, 0))
    whole = pl.BlockSpec((cols, rank), lambda i: (0, 0))
    scale = float((rows * z / rank) ** 0.5)
    momentum_next, direction = pl.pallas_call(
        functools.partial(finish, scale),
        grid=(STEPS,),
        out_shape=[
            jax.ShapeDtypeStruct((rows, cols), f32),
            jax.ShapeDtypeStruct((rows, cols), jnp.bfloat16),
        ],
        in_specs=[wide, wide, pl.BlockSpec((block, rank), lambda i: (i, 0)), whole, whole],
        out_specs=[wide, wide],
        name="finish",
    )(momentum, gradient, basis, right, following)
    return momentum_next[None], following[None], direction[None]


def solution(mesh):
    return jax.shard_map(
        functools.partial(shards, dict(mesh.shape)),
        mesh=mesh,
        in_specs=(
            P(None, "shard", ("tensor", "dp")),
            P(None, "shard", ("tensor", "dp")),
            P(None, ("tensor", "dp"), None),
        ),
        out_specs=(
            P(None, "shard", ("tensor", "dp")),
            P(None, ("tensor", "dp"), None),
            P(None, "shard", ("tensor", "dp")),
        ),
        check_vma=False,
    )
```

profile of v0, /device:TPU:0, one launch (start us, length us, event | category | flops | bytes accessed | tf_op | source)
XLA Modules:
  0.0 88.3 jit_solution(1300629623266096704)
XLA Ops:
  0.6 0.0 copy-start.3
  0.6 1.0 %copy-done.3 = f32[1,1024,128]{2,1,0:T(8,128)S(1)} copy-done((f32[1,1024,128]{2,1,0:T(8,128)S(1)}, f32[1,1024,128]{2,1,0:T(8,128)}, u32[]{:S(2)}) %copy-start.3) | copy-done | bytes 524312
  1.7 72.8 %factors.1 = (f32[2048,128]{1,0:T(8,128)S(1)}, f32[1024,128]{1,0:T(8,128)S(1)}, f32[1024,128]{1,0:T(8,128)S(1)}) custom-call(f32[2048,1024]{1,0:T(8,128)} %bitcast.8, bf16[2048,1024]{1,0:T(8,128)(2,1)} %bitcast.10, f32[1024,128]{1,0:T(8,128)S(1)} %bitcast.7), custom_call_target="tpu_custom_call" | custom-call | tf_op jit(solution)/shard_map/factors/pallas_call | solution.py:380
  74.5 0.0 copy-start
  74.5 0.8 copy-done
  75.3 0.0 copy-start.2
  75.3 1.0 %copy-done.2 = f32[2048,128]{1,0:T(8,128)} copy-done((f32[2048,128]{1,0:T(8,128)}, f32[2048,128]{1,0:T(8,128)S(1)}, u32[]{:S(2)}) %copy-start.2) | copy-done | bytes 1048600
  76.3 0.0 copy-start.4
  76.3 0.8 copy-done.4
  77.1 0.0 copy-start.1
  77.1 10.4 %finish.1 = (f32[2048,1024]{1,0:T(8,128)}, bf16[2048,1024]{1,0:T(8,128)(2,1)}) custom-call(f32[2048,1024]{1,0:T(8,128)} %bitcast.9, bf16[2048,1024]{1,0:T(8,128)(2,1)} %bitcast.11, f32[2048,128]{1,0:T(8,128)} %copy-done.2, f32[1024,128]{1,0:T(8,128)} %copy-done.4, f32[1024,128]{1,0:T(8,128)} %copy-done), custom_call_target="tpu_custom_call" | custom-call | tf_op jit(solution)/shard_map/finish/pallas_call | solution.py:425
  87.5 0.0 copy-done.1
  87.5 0.8 copy.7
Async XLA Ops:
  0.6 1.0 %copy-start.3 = (f32[1,1024,128]{2,1,0:T(8,128)S(1)}, f32[1,1024,128]{2,1,0:T(8,128)}, u32[]{:S(2)}) copy-start(f32[1,1024,128]{2,1,0:T(8,128)} %param.5) | copy-start | bytes 1572868
  74.5 0.8 copy-start
  75.3 1.0 %copy-start.2 = (f32[2048,128]{1,0:T(8,128)}, f32[2048,128]{1,0:T(8,128)S(1)}, u32[]{:S(2)}) copy-start(f32[2048,128]{1,0:T(8,128)S(1)} %get-tuple-element.8.basis_ref) | copy-start | bytes 3145732
  76.3 0.8 copy-start.4
  77.1 10.4 %copy-start.1 = (f32[1024,128]{1,0:T(8,128)S(1)}, f32[1024,128]{1,0:T(8,128)}, u32[]{:S(2)}) copy-start(f32[1024,128]{1,0:T(8,128)} %copy-done) | copy-start | bytes 1572868
where the time goes:
time: 88.5 us; the launch traced here: 88.3 us
  Pallas kernels  83.3 us (94%)
  local copies, waits for them, and re-layouts  4.39 us (5%)
    pallas_call x1, Pallas kernels, shards(): pl.pallas_call(functools.partial(factors, shape), out_shape=[jax.ShapeDty...  72.8 us
    pallas_call x1, Pallas kernels, shards(): pl.pallas_call(functools.partial(finish, scale), grid=(STEPS,), out_shape...  10.4 us
    unnamed x11, local copies, waits for them, and re-layouts  4.39 us

commit v1 on v0

--- a/solution.py
+++ b/solution.py
@@ -12,7 +12,7 @@
 decay_rate = 0.95
 epsilon = 1e-06
 CHUNKS = 8
-STEPS = 4
+STEPS = 8
 
 
 def dot(a, b, dims, precision=HIGHEST):
@@ -107,8 +107,8 @@
     return sizes, halves, orders
 
 
-def factors(shape, momentum_ref, gradient_ref, prior_ref, basis_ref, right_ref, following_ref, *scratch):
-    (mixed, raw, left, whole, local, pieces, piece_in, piece_z, piece_all, shares, share_in, squares, load_sem,
+def factors(shape, momentum_ref, gradient_ref, prior_ref, mixed, basis_ref, right_ref, following_ref, *scratch):
+    (raw, left, whole, local, pieces, piece_in, piece_z, piece_all, shares, share_in, squares, load_sem,
      gram_send, gram_recv, share_send,
      share_recv, full_send, full_recv, square_send, square_recv, prior_vmem,
      prior_sem, *stages) = scratch
@@ -338,20 +338,31 @@
     following_ref[...] = right / jnp.sqrt(mean + epsilon)
 
 
-def finish(scale, momentum_ref, gradient_ref, basis_ref, right_ref, following_ref, next_ref, direction_ref):
-    high, low = split(basis_ref[...])
-    right = right_ref[...].astype(jnp.bfloat16)
-    follow_high, follow_low = split(following_ref[...])
+def finish(scale, mixed_ref, basis_ref, right_ref, following_ref, next_ref, direction_ref, out_ref,
+           next_vmem, direction_vmem, sems):
+    rows = mixed_ref.shape[0]
+    block = rows // STEPS
+    out = pltpu.make_async_copy(following_ref, out_ref, sems.at[2, 0])
+    out.start()
+    right = (right_ref[...] * (decay_rate - 1.0)).astype(jnp.bfloat16)
+    follow = (following_ref[...] * scale).astype(jnp.bfloat16)
+    follow = jnp.concatenate([follow, follow], axis=1)
     dims = ((1,), (1,))
-    next_ref[...] = (
-        momentum_ref[...]
-        + gradient_ref[...].astype(jnp.float32)
-        - (1.0 - decay_rate) * dot(high, right, dims, None)
-    )
-    product = dot(
-        jnp.concatenate([high, low], axis=1), jnp.concatenate([follow_high, follow_high], axis=1), dims, None
-    ) + dot(high, follow_low, dims, None)
-    direction_ref[...] = (scale * product).astype(jnp.bfloat16)
+    copies = [out]
+    for i in range(STEPS):
+        at = pl.ds(i * block, block)
+        high, low = split(basis_ref[at, :])
+        next_vmem[at, :] = mixed_ref[at, :] + dot(high, right, dims, None)
+        copy = pltpu.make_async_copy(next_vmem.at[at], next_ref.at[at], sems.at[0, i])
+        copy.start()
+        copies.append(copy)
+        pair = jnp.concatenate([high, low], axis=1)
+        direction_vmem[at, :] = dot(pair, follow, dims, None).astype(jnp.bfloat16)
+        copy = pltpu.make_async_copy(direction_vmem.at[at], direction_ref.at[at], sems.at[1, i])
+        copy.start()
+        copies.append(copy)
+    for copy in copies:
+        copy.wait()
 
 
 def shards(shape, gradient, momentum, prior_right_factor):
@@ -375,19 +386,19 @@
     plane = shape["tensor"] * shape["dp"]
     dma = pltpu.SemaphoreType.DMA
     vmem = pl.BlockSpec(memory_space=pltpu.VMEM)
-    anywhere = pl.BlockSpec(memory_space=pl.ANY)
+    hbm = pl.BlockSpec(memory_space=pltpu.HBM)
     f32 = jnp.float32
-    basis, right, following = pl.pallas_call(
+    mixed, basis, right, following = pl.pallas_call(
         functools.partial(factors, shape),
         out_shape=[
-            jax.ShapeDtypeStruct((rows, rank), f32),
-            jax.ShapeDtypeStruct((cols, rank), f32),
-            jax.ShapeDtypeStruct((cols, rank), f32),
+            pltpu.VMEM((rows, cols), f32),
+            pltpu.VMEM((rows, rank), f32),
+            pltpu.VMEM((cols, rank), f32),
+            pltpu.VMEM((cols, rank), f32),
         ],
-        in_specs=[anywhere, anywhere, anywhere],
-        out_specs=[vmem, vmem, vmem],
+        in_specs=[hbm, hbm, hbm],
+        out_specs=[vmem, vmem, vmem, vmem],
         scratch_shapes=[
-            pltpu.VMEM((rows, cols), f32),
             pltpu.VMEM((rows, cols), jnp.bfloat16),
             pltpu.VMEM((rows, rank), f32),
             pltpu.VMEM((rows, rank), f32),
@@ -413,26 +424,29 @@
             *stages,
         ],
         compiler_params=pltpu.CompilerParams(
-            collective_id=0, has_side_effects=True, vmem_limit_bytes=48 * 1024 * 1024
+            collective_id=0, has_side_effects=True, vmem_limit_bytes=40 * 1024 * 1024
         ),
         name="factors",
-    )(momentum, gradient, prior)
-
-    block = rows // STEPS
-    wide = pl.BlockSpec((block, cols), lambda i: (i, 0))
-    whole = pl.BlockSpec((cols, rank), lambda i: (0, 0))
+    )(*(pltpu.with_memory_space_constraint(x, pltpu.HBM) for x in (momentum, gradient, prior)))
+
     scale = float((rows * z / rank) ** 0.5)
-    momentum_next, direction = pl.pallas_call(
+    momentum_next, direction, following = pl.pallas_call(
         functools.partial(finish, scale),
-        grid=(STEPS,),
         out_shape=[
             jax.ShapeDtypeStruct((rows, cols), f32),
             jax.ShapeDtypeStruct((rows, cols), jnp.bfloat16),
+            jax.ShapeDtypeStruct((cols, rank), f32),
         ],
-        in_specs=[wide, wide, pl.BlockSpec((block, rank), lambda i: (i, 0)), whole, whole],
-        out_specs=[wide, wide],
+        in_specs=[vmem, vmem, vmem, vmem],
+        out_specs=[hbm, hbm, hbm],
+        scratch_shapes=[
+            pltpu.VMEM((rows, cols), f32),
+            pltpu.VMEM((rows, cols), jnp.bfloat16),
+            dma((3, STEPS)),
+        ],
+        compiler_params=pltpu.CompilerParams(vmem_limit_bytes=32 * 1024 * 1024),
         name="finish",
-    )(momentum, gradient, basis, right, following)
+    )(mixed, basis, right, following)
     return momentum_next[None], following[None], direction[None]
 
 

time: 88.5 us -> 81.2 us (0.918)
  local copies, waits for them, and re-layouts: 4.39 us -> 0 us
  Pallas kernels: 83.3 us -> 80.4 us
    unnamed x11 -> x0, local copies, waits for them, and re-layouts: 4.39 us -> none
    pallas_call x2, Pallas kernels: 83.3 us -> 80.4 us  [the longest x1 75.3 us: shards(): pl.pallas_call(functools.partial(factors, shape), out_shape=[pltpu.VMEM((...]
where the time goes in v1:
time: 81.2 us; the launch traced here: 81 us
  Pallas kernels  80.4 us (99%)
    pallas_call x1, Pallas kernels, shards(): pl.pallas_call(functools.partial(factors, shape), out_shape=[pltpu.VMEM((...  75.3 us
    pallas_call x1, Pallas kernels, shards(): pl.pallas_call(functools.partial(finish, scale), out_shape=[jax.ShapeDtyp...  5.06 us

profile of v1, /device:TPU:0, one launch (start us, length us, event | category | flops | bytes accessed | tf_op | source)
XLA Modules:
  0.0 81.0 jit_solution(17844471827746336519)
XLA Ops:
  0.6 75.3 %factors.1 = (f32[2048,1024]{1,0:T(8,128)S(1)}, f32[2048,128]{1,0:T(8,128)S(1)}, f32[1024,128]{1,0:T(8,128)S(1)}, f32[1024,128]{1,0:T(8,128)S(1)}) custom-call(f32[2048,1024]{1,0:T(8,128)} %bitcast.6, bf16[2048,1024]{1,0:T(8,128)(2,1)} %bitcast.7, f32[1024,128]{1,0:T(8,128)} %bitcast.8), custom_call_target="tpu_custom_call" | custom-call | tf_op jit(solution)/shard_map/factors/pallas_call | solution.py:391
  75.9 5.1 %finish.1 = (f32[2048,1024]{1,0:T(8,128)}, bf16[2048,1024]{1,0:T(8,128)(2,1)}, f32[1024,128]{1,0:T(8,128)}) custom-call(f32[2048,1024]{1,0:T(8,128)S(1)} %get-tuple-element.10.mixed_ref, f32[2048,128]{1,0:T(8,128)S(1)} %get-tuple-element.11.basis_ref, f32[1024,128]{1,0:T(8,128)S(1)} %get-tuple-element.12.right_ref, ...), custom_call_target="tpu_custom_call" | custom-call | tf_op jit(solution)/shard_map/finish/pallas_call | solution.py:433

commit v2 on v1

v2 whole, which is shorter than its diff:
```python
import functools

import jax
import jax.numpy as jnp
from jax import lax
from jax.experimental import pallas as pl
from jax.experimental.pallas import tpu as pltpu
from jax.sharding import PartitionSpec as P

MESH = pl.DeviceIdType.MESH
HIGHEST = lax.Precision.HIGHEST
decay_rate = 0.95
epsilon = 1e-06
STEPS = 8
MiB = 1024 * 1024
ROWS, NORMAL, TURNED = ((0,), (0,)), ((1,), (0,)), ((1,), (1,))


def dot(a, b, dims, precision=None):
    return lax.dot_general(
        a, b, (dims, ((), ())), precision=precision, preferred_element_type=jnp.float32
    )


def split(value):
    high = value.astype(jnp.bfloat16)
    low = (value - high.astype(jnp.float32)).astype(jnp.bfloat16)
    return high, low


def split3(value):
    high = value.astype(jnp.bfloat16)
    rest = value - high.astype(jnp.float32)
    middle = rest.astype(jnp.bfloat16)
    return high, middle, (rest - middle.astype(jnp.float32)).astype(jnp.bfloat16)


def inverse_steps(a, start, stop):
    size = a.shape[0]
    sub = lax.broadcasted_iota(jnp.int32, (8, size), 0)
    lane = lax.broadcasted_iota(jnp.int32, (8, size), 1)
    rows = lax.broadcasted_iota(jnp.int32, (size, size), 0)
    lanes = lax.broadcasted_iota(jnp.int32, (size, size), 1)

    def row(value, index):
        return jnp.broadcast_to(value[index : index + 1], value.shape)

    def block(step, a):
        top = a[:8]
        columns = [jnp.broadcast_to(top[:, c : c + 1], (8, size)) for c in range(8)]
        panel = jnp.where(lane < 8, jnp.where(lane == sub, 1.0, 0.0), top)
        scale = jnp.zeros((8, size), jnp.float32)
        for c in range(8):
            inverse_root = lax.rsqrt(row(columns[c], c))
            scale = jnp.where(sub == c, inverse_root, scale)
            factor = jnp.where(sub > c, columns[c] * (inverse_root * inverse_root), 0.0)
            panel = panel - factor * row(panel, c)
            for j in range(c + 1, 8):
                columns[j] = columns[j] - factor * row(columns[j], c)
        square = scale * scale
        solved = panel * square
        for c in range(7, 0, -1):
            solved = solved - jnp.where(sub < c, columns[c] * square, 0.0) * row(solved, c)
        active = rows < size - 8 * step
        source = jnp.where(active, a, 0.0)[8:]
        rest = jnp.where(active & (lanes < 8), 0.0, a)[8:]
        for c in range(8):
            rest = rest - jnp.broadcast_to(source[:, c : c + 1], rest.shape) * jnp.broadcast_to(
                solved[c : c + 1], rest.shape
            )
        return pltpu.roll(jnp.concatenate([rest, panel * scale], axis=0), size - 8, 1)

    return lax.fori_loop(start, stop, block, a)


def lower(a):
    rows = lax.broadcasted_iota(jnp.int32, a.shape, 0)
    lanes = lax.broadcasted_iota(jnp.int32, a.shape, 1)
    return jnp.where(rows >= lanes, a, 0.0)


def remote(src, dst, send_sem, recv_sem, device):
    return pltpu.make_async_remote_copy(
        src_ref=src, dst_ref=dst, send_sem=send_sem, recv_sem=recv_sem, device_id=device, device_id_type=MESH
    )


def widths(cols):
    group = 256 if cols % 256 == 0 else cols
    chunk = 128 if group % 128 == 0 else group
    return group, chunk


def factors(shape, momentum_ref, gradient_ref, prior_ref, mixed, pair_ref, right_ref, following_ref,
            raw, wide_high, wide_low, prior_vmem, left, core_in, plane_in, whole, turned, value_t, sums, totals,
            arrive, pieces, piece_in, piece_z, piece_all, squares, load_sem, prior_sem, core_send, core_recv,
            plane_send, plane_recv, ag_send, ag_recv, half_sem, gram_send, gram_recv, chain_send, chain_recv,
            square_send, square_recv):
    rows, cols = mixed.shape
    rank = prior_ref.shape[1]
    depth, dp = shape["shard"], shape["dp"]
    cores = 2 if shape["tensor"] % 2 == 0 else 1
    nx = shape["tensor"] // cores
    chips = nx * dp
    plane = chips * cores
    own = rows // plane
    s, t, y = lax.axis_index("shard"), lax.axis_index("tensor"), lax.axis_index("dp")
    core, x = lax.rem(t, cores), lax.div(t, cores)
    me = t * dp + y

    def chip(offset):
        px = lax.rem(x + lax.div(offset, dp), nx)
        py = lax.rem(y + lax.rem(offset, dp), dp)
        return px * dp + py, {"tensor": px * cores + core, "dp": py}

    def place(half, index):
        return pl.ds(pl.multiple_of((half * chips + index) * own, 8), own)

    def peer(k):
        other = lax.rem(me + k, plane)
        return other, {"tensor": lax.div(other, dp), "dp": lax.rem(other, dp)}

    def across(k):
        other = lax.rem(s + k, depth)
        return other, {"shard": other}

    partner = {"tensor": x * cores + cores - 1 - core}
    halves = (core,) if cores == 1 else (1 - core, core)

    def load(slot, at):
        return (
            pltpu.make_async_copy(momentum_ref.at[at], mixed.at[at], load_sem.at[0, slot]),
            pltpu.make_async_copy(gradient_ref.at[at], raw.at[at], load_sem.at[1, slot]),
        )

    prior_copy = pltpu.make_async_copy(prior_ref, prior_vmem, prior_sem)
    prior_copy.start()
    for h, half in enumerate(halves):
        for i in range(chips):
            for copy in load(h * chips + i, place(half, chip(chips - 1 - i)[0])):
                copy.start()

    barrier = pltpu.get_barrier_semaphore()
    for k in range(1, plane):
        pl.semaphore_signal(barrier, inc=1, device_id=peer(k)[1], device_id_type=MESH)
    for k in range(1, depth):
        pl.semaphore_signal(barrier, inc=1, device_id=across(k)[1], device_id_type=MESH)

    half_depth = max(depth // 2, 1)
    first = s < half_depth
    level = jnp.where(first, s, depth - 1 - s)
    outer = level > 0
    middle = level == half_depth - 1
    step_in = jnp.where(first, 1, -1)
    group, chunk = widths(cols)
    count = cols // chunk

    prior_copy.wait()
    prior_pair = jnp.concatenate(split(prior_vmem[...]), axis=1)
    pl.semaphore_wait(barrier, plane + depth - 2)

    def product(slot, at):
        for copy in load(slot, at):
            copy.wait()
        value = mixed[at, :] + raw[at, :].astype(jnp.float32)
        mixed[at, :] = value
        high, low = split(value)
        wide_high[at, :] = high
        wide_low[at, :] = low
        both = dot(high, prior_pair, NORMAL) + dot(low, prior_pair, NORMAL)
        return both[:, :rank] + both[:, rank:]

    def core_copy(i):
        at = place(cores - 1 - core, chip(chips - 1 - i)[0])
        return remote(left.at[at], core_in.at[i], core_send.at[i], core_recv.at[i], partner)

    def plane_copy(offset):
        index, device = chip(offset)
        slot = offset - 1
        return remote(left.at[place(core, index)], plane_in.at[slot], plane_send.at[slot], plane_recv.at[slot], device)

    if cores == 2:

        def outgoing(i, carry):
            at = place(1 - core, chip(chips - 1 - i)[0])
            left[at, :] = product(i, at)
            core_copy(i).start()
            return carry

        with jax.named_scope("p1_other"):
            lax.fori_loop(0, chips, outgoing, 0)

    def kept(i, carry):
        offset = chips - 1 - i
        at = place(core, chip(offset)[0])
        value = product((cores - 1) * chips + i, at)
        if cores == 2:
            core_copy(i).wait_recv()
            value = value + core_in[i]
        left[at, :] = value

        @pl.when(offset > 0)
        def _():
            plane_copy(offset).start()

        return carry

    with jax.named_scope("p2_own"):
        lax.fori_loop(0, chips, kept, 0)

    mine = place(core, x * dp + y)
    with jax.named_scope("p3_rswait"):
        total = left[mine, :]
        for offset in range(1, chips):
            plane_copy(offset).wait_recv()
            total = total + plane_in[offset - 1]
        whole[mine, :] = total

    piece = rank // plane

    def summed(slots, n):
        value = slots[0]
        for i in range(1, n):
            value = value + slots[i]
        return value

    def gram_sends(turn, stage, n, find, source, target):
        copies = []
        for k in range(1, n):
            other, device = find(k)
            copy = remote(source(other), target, gram_send.at[turn, stage, k - 1],
                          gram_recv.at[turn, stage, k - 1], device)
            copy.start()
            copies.append(copy)
        return copies

    def gram_steps(turn, gram):
        for i in range(plane):
            pieces[turn, i] = gram[i * piece : (i + 1) * piece]
        piece_in[turn, me] = pieces[turn, me]
        copies = gram_sends(turn, 0, plane, peer, lambda i: pieces.at[turn, i], piece_in.at[turn, me])
        yield
        for copy in copies:
            copy.wait()
        piece_z[turn, s] = summed(piece_in.at[turn], plane)
        mine_z = piece_z.at[turn, s]
        copies = gram_sends(turn, 1, depth, across, lambda i: mine_z, mine_z)
        yield
        for copy in copies:
            copy.wait()
        piece_all[turn, me] = summed(piece_z.at[turn], depth)
        mine_all = piece_all.at[turn, me]
        copies = gram_sends(turn, 2, plane, peer, lambda i: mine_all, mine_all)
        yield
        for copy in copies:
            copy.wait()
        yield jnp.concatenate([piece_all[turn, i] for i in range(plane)], axis=0)

    with jax.named_scope("p4_gram"):
        steps = gram_steps(0, dot(total, total, ROWS, HIGHEST))
        next(steps)
    spread = []
    for offset in range(1, chips):
        copy = remote(whole.at[mine], whole.at[mine], ag_send.at[offset - 1], ag_recv.at[offset - 1], chip(offset)[1])
        copy.start()
        spread.append(copy)
    with jax.named_scope("p5_gram1"):
        next(steps)
    with jax.named_scope("p6_gram2"):
        next(steps)
    with jax.named_scope("p7_agwait"):
        for offset in range(1, chips):
            plane_copy(offset).wait_send()
        for copy in spread:
            copy.wait()
        if cores == 2:
            for i in range(chips):
                core_copy(i).wait_send()
            at = pl.ds(pl.multiple_of(core * (rows // 2), 8), rows // 2)
            half_copy = remote(whole.at[at], whole.at[at], half_sem.at[0], half_sem.at[1], partner)
            half_copy.start()
    with jax.named_scope("p8_gram3"):
        gram = next(steps)
    with jax.named_scope("p9_inv1"):
        inverse = lower(inverse_steps(gram, 0, rank // 8))
    with jax.named_scope("q0_value"):
        if cores == 2:
            half_copy.wait()
        w_high, w_middle, w_low = split3(inverse)
        ends = jnp.concatenate(
            [jnp.concatenate([w_high, w_middle], axis=1), jnp.concatenate([w_middle, w_high], axis=1)], axis=0
        )
        tail = jnp.concatenate([w_low, w_high], axis=1)
        for i in range(STEPS):
            block = rows // STEPS
            at = slice(i * block, (i + 1) * block)
            high, middle_part, low = split3(whole[at, :])
            both = dot(ends, jnp.concatenate([high, middle_part], axis=1), TURNED)
            value = both[:rank] + (both[rank:] + dot(tail, jnp.concatenate([high, low], axis=1), TURNED))
            value_t[:, at] = value
            high, low = split(value)
            turned[:rank, at] = high
            turned[rank:, at] = low
    with jax.named_scope("q1_gram"):
        begin = pl.multiple_of((core * chips + x * dp + y) * own, 128 if own % 128 == 0 else 8)
        if own % 128 == 0:
            part = value_t[:, pl.ds(begin, own)]
            gram = dot(part, part, TURNED, HIGHEST)
        else:
            part = dot(whole[mine, :], inverse, TURNED, HIGHEST)
            gram = dot(part, part, ROWS, HIGHEST)
        steps = gram_steps(1, gram)
        next(steps)

    def inward(c):
        slot = jnp.where(middle, 1, 0)
        return remote(sums.at[c], arrive.at[slot, c], chain_send.at[0, c], chain_recv.at[slot, c],
                      {"shard": s + step_in})

    def outward(c):
        return remote(totals.at[c], arrive.at[1, c], chain_send.at[1, c], chain_recv.at[1, c],
                      {"shard": s - step_in})

    def landed(slot, c):
        return remote(sums.at[c], arrive.at[slot, c], chain_send.at[0, c], chain_recv.at[slot, c],
                      {"shard": s + step_in})

    def near(c):
        if depth > 1:

            @pl.when(outer)
            def _():
                landed(0, c).wait_recv()
                sums[c] = sums[c] + arrive[0, c]
                inward(c).start()

    def far(c):
        if depth > 1:
            landed(1, c).wait_recv()
            totals[c] = jnp.where(middle, sums[c] + arrive[1, c], arrive[1, c])

            @pl.when(outer)
            def _():
                outward(c).start()
        else:
            totals[c] = sums[c]

    per = group // chunk
    groups = cols // group
    with jax.named_scope("q2_right"):
        for g in range(groups):
            at = slice(g * group, (g + 1) * group)
            both = dot(turned[...], wide_high[:, at], NORMAL)
            value = both[:rank] + both[rank:] + dot(turned[:rank], wide_low[:, at], NORMAL)
            for i in range(per):
                c = g * per + i
                sums[c] = value[:, i * chunk : (i + 1) * chunk]
                if depth > 1:

                    @pl.when(jnp.logical_not(outer))
                    def _():
                        inward(c).start()

            if g == min(1, groups - 1):
                with jax.named_scope("q2_gram1"):
                    next(steps)

    blocks = rank // 8
    state = {}

    def gram_second():
        with jax.named_scope("q4_gram2"):
            next(steps)

    def gram_third():
        with jax.named_scope("q4_gram3"):
            state["a"] = next(steps)
            state["at"] = 0

    def invert(share):
        with jax.named_scope("q5_inv2"):
            stop = min(state["at"] + share, blocks)
            state["a"] = inverse_steps(state["a"], state["at"], stop)
            state["at"] = stop

    def correct(c):
        with jax.named_scope("q7_right"):
            value = dot(totals[c], state["inverse"], ((0,), (1,)), HIGHEST)
            right_ref[c * chunk : (c + 1) * chunk, :] = value
            state["squares"] = state.get("squares", 0.0) + jnp.sum(value * value, axis=0, keepdims=True)

    def basis():
        with jax.named_scope("q6_basis"):
            inverse = state["inverse"]
            high, low = split(inverse)
            left_pair = jnp.concatenate([high, low], axis=1)
            for i in range(STEPS):
                block = rows // STEPS
                at = slice(i * block, (i + 1) * block)
                value = dot(
                    left_pair, jnp.concatenate([turned[:rank, at], turned[:rank, at]], axis=0), NORMAL
                ) + dot(high, turned[rank:, at], NORMAL)
                high_t, low_t = split(value.T)
                pair_ref[at, :rank] = high_t
                pair_ref[at, rank:] = low_t

    lag = min(3, count - 1)
    with jax.named_scope("q3_near"):
        for c in range(lag):
            near(c)
    gram_second()
    with jax.named_scope("q3_chain"):
        done = 0
        for c in range(count):
            if c + lag < count:
                near(c + lag)
            if c == min(3, count - 1):
                gram_third()
            if "a" in state and state["at"] < blocks:
                invert(-(-blocks // min(4, count)) if c < count - 1 else blocks)
                if state["at"] == blocks and "inverse" not in state:
                    state["inverse"] = lower(state["a"])
                    basis()
            far(c)
            if "inverse" in state:
                while done <= c:
                    correct(done)
                    done += 1
    with jax.named_scope("q8_squares"):
        squares[me] = jnp.broadcast_to(state["squares"], (8, rank))
        copies = []
        for k in range(1, plane):
            copy = remote(squares.at[me], squares.at[me], square_send.at[k - 1], square_recv.at[k - 1], peer(k)[1])
            copy.start()
            copies.append(copy)
    with jax.named_scope("q9_momentum"):
        scaled = (right_ref[...] * (decay_rate - 1.0)).astype(jnp.bfloat16)

        def update(i, carry):
            block = rows // STEPS
            at = pl.ds(pl.multiple_of(i * block, 8), block)
            mixed[at, :] = mixed[at, :] + dot(pair_ref[at, :rank], scaled, TURNED)
            return carry

        lax.fori_loop(0, STEPS, update, 0)
    with jax.named_scope("r0_follow"):
        for copy in copies:
            copy.wait()
        mean = summed(squares, plane)[:1] / (cols * plane)
        following_ref[...] = right_ref[...] / jnp.sqrt(mean + epsilon)
        if depth > 1:
            for c in range(count):
                inward(c).wait_send()

            @pl.when(outer)
            def _():
                for c in range(count):
                    outward(c).wait_send()


def finish(scale, mixed_ref, pair_ref, following_ref, next_ref, direction_ref, out_ref, direction_vmem, sems):
    rows = mixed_ref.shape[0]
    rank = following_ref.shape[1]
    block = rows // STEPS
    copies = [pltpu.make_async_copy(following_ref, out_ref, sems.at[2, 0])]
    for i in range(STEPS):
        at = pl.ds(i * block, block)
        copies.append(pltpu.make_async_copy(mixed_ref.at[at], next_ref.at[at], sems.at[0, i]))
    for copy in copies:
        copy.start()
    high, low = split(following_ref[...] * scale)
    follow = jnp.concatenate([high, high], axis=1)
    for i in range(STEPS):
        at = pl.ds(i * block, block)
        value = dot(pair_ref[at, :], follow, TURNED) + dot(pair_ref[at, :rank], low, TURNED)
        direction_vmem[at, :] = value.astype(jnp.bfloat16)
        copy = pltpu.make_async_copy(direction_vmem.at[at], direction_ref.at[at], sems.at[1, i])
        copy.start()
        copies.append(copy)
    for copy in copies:
        copy.wait()


def shards(shape, gradient, momentum, prior_right_factor):
    gradient, momentum, prior = gradient[0], momentum[0], prior_right_factor[0]
    rows, cols = momentum.shape
    rank = prior.shape[1]
    z = shape["shard"]
    plane = shape["tensor"] * shape["dp"]
    cores = 2 if shape["tensor"] % 2 == 0 else 1
    chips = plane // cores
    own = rows // plane
    group, chunk = widths(cols)
    count = cols // chunk
    dma = pltpu.SemaphoreType.DMA
    vmem = pl.BlockSpec(memory_space=pltpu.VMEM)
    hbm = pl.BlockSpec(memory_space=pltpu.HBM)
    f32, bf16 = jnp.float32, jnp.bfloat16
    others = max(chips - 1, 1)
    most = max(plane, z)
    mixed, pair, right, following = pl.pallas_call(
        functools.partial(factors, shape),
        out_shape=[
            pltpu.VMEM((rows, cols), f32),
            pltpu.VMEM((rows, 2 * rank), bf16),
            pltpu.VMEM((cols, rank), f32),
            pltpu.VMEM((cols, rank), f32),
        ],
        in_specs=[hbm, hbm, hbm],
        out_specs=[vmem, vmem, vmem, vmem],
        scratch_shapes=[
            pltpu.VMEM((rows, cols), bf16),
            pltpu.VMEM((rows, cols), bf16),
            pltpu.VMEM((rows, cols), bf16),
            pltpu.VMEM((cols, rank), f32),
            pltpu.VMEM((rows, rank), f32),
            pltpu.VMEM((chips, own, rank), f32),
            pltpu.VMEM((others, own, rank), f32),
            pltpu.VMEM((rows, rank), f32),
            pltpu.VMEM((2 * rank, rows), bf16),
            pltpu.VMEM((rank, rows), f32),
            pltpu.VMEM((count, rank, chunk), f32),
            pltpu.VMEM((count, rank, chunk), f32),
            pltpu.VMEM((2, count, rank, chunk), f32),
            pltpu.VMEM((2, plane, rank // plane, rank), f32),
            pltpu.VMEM((2, plane, rank // plane, rank), f32),
            pltpu.VMEM((2, z, rank // plane, rank), f32),
            pltpu.VMEM((2, plane, rank // plane, rank), f32),
            pltpu.VMEM((plane, 8, rank), f32),
            dma((2, plane)),
            dma,
            dma((chips,)),
            dma((chips,)),
            dma((others,)),
            dma((others,)),
            dma((others,)),
            dma((others,)),
            dma((2,)),
            dma((2, 3, most)),
            dma((2, 3, most)),
            dma((2, count)),
            dma((2, count)),
            dma((most,)),
            dma((most,)),
        ],
        compiler_params=pltpu.CompilerParams(
            collective_id=0, has_side_effects=True, vmem_limit_bytes=36 * MiB
        ),
        name="factors",
    )(*(pltpu.with_memory_space_constraint(x, pltpu.HBM) for x in (momentum, gradient, prior)))

    scale = float((rows * z / rank) ** 0.5)
    momentum_next, direction, following = pl.pallas_call(
        functools.partial(finish, scale),
        out_shape=[
            jax.ShapeDtypeStruct((rows, cols), f32),
            jax.ShapeDtypeStruct((rows, cols), bf16),
            jax.ShapeDtypeStruct((cols, rank), f32),
        ],
        in_specs=[vmem, vmem, vmem],
        out_specs=[hbm, hbm, hbm],
        scratch_shapes=[pltpu.VMEM((rows, cols), bf16), dma((3, STEPS))],
        compiler_params=pltpu.CompilerParams(vmem_limit_bytes=24 * MiB),
        name="finish",
    )(mixed, pair, following)
    return momentum_next[None], following[None], direction[None]


def solution(mesh):
    return jax.shard_map(
        functools.partial(shards, dict(mesh.shape)),
        mesh=mesh,
        in_specs=(
            P(None, "shard", ("tensor", "dp")),
            P(None, "shard", ("tensor", "dp")),
            P(None, ("tensor", "dp"), None),
        ),
        out_specs=(
            P(None, "shard", ("tensor", "dp")),
            P(None, ("tensor", "dp"), None),
            P(None, "shard", ("tensor", "dp")),
        ),
        check_vma=False,
    )
```

time: 81.2 us -> 72 us (0.89)
  Pallas kernels: 80.4 us -> 71.2 us
    pallas_call x1, Pallas kernels: 75.3 us -> 66.3 us  [shards(): pl.pallas_call(functools.partial(factors, shape), out_shape=[pltpu.VMEM((...]
where the time goes in v2:
time: 72 us; the launch traced here: 71.8 us
  Pallas kernels  71.2 us (99%)
    pallas_call x1, Pallas kernels, shards(): pl.pallas_call(functools.partial(factors, shape), out_shape=[pltpu.VMEM((...  66.3 us
    pallas_call x1, Pallas kernels, shards(): pl.pallas_call(functools.partial(finish, scale), out_shape=[jax.ShapeDtyp...  4.92 us

profile of v2, /device:TPU:0, one launch (start us, length us, event | category | flops | bytes accessed | tf_op | source)
XLA Modules:
  0.0 71.8 jit_solution(8420454380766300554)
XLA Ops:
  0.6 66.3 %factors.1 = (f32[2048,1024]{1,0:T(8,128)S(1)}, bf16[2048,256]{1,0:T(8,128)(2,1)S(1)}, f32[1024,128]{1,0:T(8,128)}, f32[1024,128]{1,0:T(8,128)S(1)}) custom-call(f32[2048,1024]{1,0:T(8,128)} %bitcast.6, bf16[2048,1024]{1,0:T(8,128)(2,1)} %bitcast.7, f32[1024,128]{1,0:T(8,128)} %bitcast.8), custom_call_target="tpu_custom_call" | custom-call | tf_op jit(solution)/shard_map/factors/pallas_call | solution.py:501
  66.9 4.9 %finish.1 = (f32[2048,1024]{1,0:T(8,128)}, bf16[2048,1024]{1,0:T(8,128)(2,1)}, f32[1024,128]{1,0:T(8,128)}) custom-call(f32[2048,1024]{1,0:T(8,128)S(1)} %get-tuple-element.9.mixed_ref, bf16[2048,256]{1,0:T(8,128)(2,1)S(1)} %get-tuple-element.10.pair_ref, f32[1024,128]{1,0:T(8,128)S(1)} %get-tuple-element.11.following_ref), custom_call_target="tpu_custom_call" | custom-call | tf_op jit(solution)/shard_map/finish/pallas_call | solution.py:553

commit v3 on v2

--- a/solution.py
+++ b/solution.py
@@ -12,6 +12,10 @@
 decay_rate = 0.95
 epsilon = 1e-06
 STEPS = 8
+AHEAD = 3
+LAG = 5
+THIRD = 4
+SHARE = 1
 MiB = 1024 * 1024
 ROWS, NORMAL, TURNED = ((0,), (0,)), ((1,), (0,)), ((1,), (1,))
 
@@ -92,8 +96,8 @@
 
 
 def factors(shape, momentum_ref, gradient_ref, prior_ref, mixed, pair_ref, right_ref, following_ref,
-            raw, wide_high, wide_low, prior_vmem, left, core_in, plane_in, whole, turned, value_t, sums, totals,
-            arrive, pieces, piece_in, piece_z, piece_all, squares, load_sem, prior_sem, core_send, core_recv,
+            raw, wide_high, wide_low, prior_vmem, prior_pair, left, core_in, plane_in, whole, turned, value_t, sums, totals,
+            arrive, pieces, piece_in, piece_z, piece_all, squares, work, load_sem, prior_sem, core_send, core_recv,
             plane_send, plane_recv, ag_send, ag_recv, half_sem, gram_send, gram_recv, chain_send, chain_recv,
             square_send, square_recv):
     rows, cols = mixed.shape
@@ -125,7 +129,6 @@
         return other, {"shard": other}
 
     partner = {"tensor": x * cores + cores - 1 - core}
-    halves = (core,) if cores == 1 else (1 - core, core)
 
     def load(slot, at):
         return (
@@ -133,12 +136,18 @@
             pltpu.make_async_copy(gradient_ref.at[at], raw.at[at], load_sem.at[1, slot]),
         )
 
+    loads = chips * cores
+
+    def spot(slot):
+        i = lax.div(slot, cores)
+        half = lax.rem(core + 1 + lax.rem(slot, cores), cores)
+        return place(half, chip(chips - 1 - i)[0])
+
     prior_copy = pltpu.make_async_copy(prior_ref, prior_vmem, prior_sem)
     prior_copy.start()
-    for h, half in enumerate(halves):
-        for i in range(chips):
-            for copy in load(h * chips + i, place(half, chip(chips - 1 - i)[0])):
-                copy.start()
+    for slot in range(min(AHEAD, loads)):
+        for copy in load(slot, spot(slot)):
+            copy.start()
 
     barrier = pltpu.get_barrier_semaphore()
     for k in range(1, plane):
@@ -156,18 +165,27 @@
     count = cols // chunk
 
     prior_copy.wait()
-    prior_pair = jnp.concatenate(split(prior_vmem[...]), axis=1)
+    high, low = split(prior_vmem[...])
+    prior_pair[:, :rank] = high
+    prior_pair[:, rank:] = low
     pl.semaphore_wait(barrier, plane + depth - 2)
 
     def product(slot, at):
         for copy in load(slot, at):
             copy.wait()
+        ahead = slot + AHEAD
+
+        @pl.when(ahead < loads)
+        def _():
+            for copy in load(ahead, spot(ahead)):
+                copy.start()
+
         value = mixed[at, :] + raw[at, :].astype(jnp.float32)
         mixed[at, :] = value
         high, low = split(value)
         wide_high[at, :] = high
         wide_low[at, :] = low
-        both = dot(high, prior_pair, NORMAL) + dot(low, prior_pair, NORMAL)
+        both = dot(high, prior_pair[...], NORMAL) + dot(low, prior_pair[...], NORMAL)
         return both[:, :rank] + both[:, rank:]
 
     def core_copy(i):
@@ -179,37 +197,36 @@
         slot = offset - 1
         return remote(left.at[place(core, index)], plane_in.at[slot], plane_send.at[slot], plane_recv.at[slot], device)
 
-    if cores == 2:
-
-        def outgoing(i, carry):
-            at = place(1 - core, chip(chips - 1 - i)[0])
-            left[at, :] = product(i, at)
-            core_copy(i).start()
-            return carry
-
-        with jax.named_scope("p1_other"):
-            lax.fori_loop(0, chips, outgoing, 0)
-
-    def kept(i, carry):
+    def settle(i):
         offset = chips - 1 - i
         at = place(core, chip(offset)[0])
-        value = product((cores - 1) * chips + i, at)
         if cores == 2:
             core_copy(i).wait_recv()
-            value = value + core_in[i]
-        left[at, :] = value
-
-        @pl.when(offset > 0)
+            left[at, :] = left[at, :] + core_in[i]
+        return offset
+
+    def partial(slot, carry):
+        i = lax.div(slot, cores)
+        at = spot(slot)
+        left[at, :] = product(slot, at)
+        if cores == 2:
+
+            @pl.when(lax.rem(slot, cores) == 0)
+            def _():
+                core_copy(i).start()
+
+        @pl.when(jnp.logical_and(lax.rem(slot, cores) == 0, slot > 0))
         def _():
-            plane_copy(offset).start()
+            plane_copy(settle(i - 1)).start()
 
         return carry
 
-    with jax.named_scope("p2_own"):
-        lax.fori_loop(0, chips, kept, 0)
+    with jax.named_scope("p1_left"):
+        lax.fori_loop(0, loads, partial, 0)
 
     mine = place(core, x * dp + y)
     with jax.named_scope("p3_rswait"):
+        settle(chips - 1)
         total = left[mine, :]
         for offset in range(1, chips):
             plane_copy(offset).wait_recv()
@@ -251,10 +268,12 @@
         piece_all[turn, me] = summed(piece_z.at[turn], depth)
         mine_all = piece_all.at[turn, me]
         copies = gram_sends(turn, 2, plane, peer, lambda i: mine_all, mine_all)
-        yield
+        yield copies
+
+    def gram_whole(turn, copies):
         for copy in copies:
             copy.wait()
-        yield jnp.concatenate([piece_all[turn, i] for i in range(plane)], axis=0)
+        return jnp.concatenate([piece_all[turn, i] for i in range(plane)], axis=0)
 
     with jax.named_scope("p4_gram"):
         steps = gram_steps(0, dot(total, total, ROWS, HIGHEST))
@@ -267,7 +286,7 @@
     with jax.named_scope("p5_gram1"):
         next(steps)
     with jax.named_scope("p6_gram2"):
-        next(steps)
+        last = next(steps)
     with jax.named_scope("p7_agwait"):
         for offset in range(1, chips):
             plane_copy(offset).wait_send()
@@ -280,7 +299,7 @@
             half_copy = remote(whole.at[at], whole.at[at], half_sem.at[0], half_sem.at[1], partner)
             half_copy.start()
     with jax.named_scope("p8_gram3"):
-        gram = next(steps)
+        gram = gram_whole(0, last)
     with jax.named_scope("p9_inv1"):
         inverse = lower(inverse_steps(gram, 0, rank // 8))
     with jax.named_scope("q0_value"):
@@ -312,38 +331,46 @@
         steps = gram_steps(1, gram)
         next(steps)
 
-    def inward(c):
+    parts = 2 if rank % 16 == 0 else 1
+    tall = rank // parts
+    units = count * parts
+
+    def unit(ref, u):
+        return ref.at[u // parts, pl.ds((u % parts) * tall, tall)]
+
+    def inward(u):
         slot = jnp.where(middle, 1, 0)
-        return remote(sums.at[c], arrive.at[slot, c], chain_send.at[0, c], chain_recv.at[slot, c],
+        return remote(unit(sums, u), unit(arrive.at[slot], u), chain_send.at[0, u], chain_recv.at[slot, u],
                       {"shard": s + step_in})
 
-    def outward(c):
-        return remote(totals.at[c], arrive.at[1, c], chain_send.at[1, c], chain_recv.at[1, c],
+    def outward(u):
+        return remote(unit(totals, u), unit(arrive.at[1], u), chain_send.at[1, u], chain_recv.at[1, u],
                       {"shard": s - step_in})
 
-    def landed(slot, c):
-        return remote(sums.at[c], arrive.at[slot, c], chain_send.at[0, c], chain_recv.at[slot, c],
-                      {"shard": s + step_in})
-
-    def near(c):
+    def landed(slot, u):
+        remote(unit(sums, u), unit(arrive.at[slot], u), chain_send.at[0, u], chain_recv.at[slot, u],
+               {"shard": s + step_in}).wait_recv()
+
+    def near(u):
         if depth > 1:
 
             @pl.when(outer)
             def _():
-                landed(0, c).wait_recv()
-                sums[c] = sums[c] + arrive[0, c]
-                inward(c).start()
-
-    def far(c):
+                landed(0, u)
+                unit(sums, u)[...] = unit(sums, u)[...] + unit(arrive.at[0], u)[...]
+                inward(u).start()
+
+    def far(u):
         if depth > 1:
-            landed(1, c).wait_recv()
-            totals[c] = jnp.where(middle, sums[c] + arrive[1, c], arrive[1, c])
+            landed(1, u)
+            got = unit(arrive.at[1], u)[...]
+            unit(totals, u)[...] = jnp.where(middle, unit(sums, u)[...] + got, got)
 
             @pl.when(outer)
             def _():
-                outward(c).start()
+                outward(u).start()
         else:
-            totals[c] = sums[c]
+            unit(totals, u)[...] = unit(sums, u)[...]
 
     per = group // chunk
     groups = cols // group
@@ -353,46 +380,36 @@
             both = dot(turned[...], wide_high[:, at], NORMAL)
             value = both[:rank] + both[rank:] + dot(turned[:rank], wide_low[:, at], NORMAL)
             for i in range(per):
-                c = g * per + i
-                sums[c] = value[:, i * chunk : (i + 1) * chunk]
-                if depth > 1:
-
-                    @pl.when(jnp.logical_not(outer))
-                    def _():
-                        inward(c).start()
-
+                sums[g * per + i] = value[:, i * chunk : (i + 1) * chunk]
             if g == min(1, groups - 1):
                 with jax.named_scope("q2_gram1"):
                     next(steps)
+            if depth > 1:
+
+                @pl.when(jnp.logical_not(outer))
+                def _():
+                    for u in range(g * per * parts, (g + 1) * per * parts):
+                        inward(u).start()
+
+    lag = min(LAG, units)
+    last = None
+    for u in range(lag):
+        if u == max(lag - 2, 0):
+            with jax.named_scope("q4_gram2"):
+                last = next(steps)
+        with jax.named_scope("q3_near"):
+            near(u)
 
     blocks = rank // 8
-    state = {}
-
-    def gram_second():
-        with jax.named_scope("q4_gram2"):
-            next(steps)
-
-    def gram_third():
-        with jax.named_scope("q4_gram3"):
-            state["a"] = next(steps)
-            state["at"] = 0
-
-    def invert(share):
+
+    def invert(start, stop):
         with jax.named_scope("q5_inv2"):
-            stop = min(state["at"] + share, blocks)
-            state["a"] = inverse_steps(state["a"], state["at"], stop)
-            state["at"] = stop
-
-    def correct(c):
-        with jax.named_scope("q7_right"):
-            value = dot(totals[c], state["inverse"], ((0,), (1,)), HIGHEST)
-            right_ref[c * chunk : (c + 1) * chunk, :] = value
-            state["squares"] = state.get("squares", 0.0) + jnp.sum(value * value, axis=0, keepdims=True)
+            work[...] = inverse_steps(work[...], start, stop)
 
     def basis():
         with jax.named_scope("q6_basis"):
-            inverse = state["inverse"]
-            high, low = split(inverse)
+            work[...] = lower(work[...])
+            high, low = split(work[...])
             left_pair = jnp.concatenate([high, low], axis=1)
             for i in range(STEPS):
                 block = rows // STEPS
@@ -404,30 +421,49 @@
                 pair_ref[at, :rank] = high_t
                 pair_ref[at, rank:] = low_t
 
-    lag = min(3, count - 1)
-    with jax.named_scope("q3_near"):
-        for c in range(lag):
-            near(c)
-    gram_second()
-    with jax.named_scope("q3_chain"):
-        done = 0
+    def correct(c):
+        with jax.named_scope("q7_right"):
+            value = dot(totals[c], work[...], ((0,), (1,)), HIGHEST)
+            right_ref[c * chunk : (c + 1) * chunk, :] = value
+            column = jnp.sum(value * value, axis=0, keepdims=True)
+            squares[me] = squares[me] + jnp.broadcast_to(column, (8, rank))
+
+    squares[me] = jnp.zeros((8, rank), jnp.float32)
+
+    @pl.when(outer)
+    def _():
+        third = min(THIRD, units - 1)
+        at = 0
+        for u in range(units):
+            with jax.named_scope("q3_far"):
+                far(u)
+            if u + lag < units:
+                with jax.named_scope("q3_near2"):
+                    near(u + lag)
+            if u == third:
+                with jax.named_scope("q4_gram3"):
+                    work[...] = gram_whole(1, last)
+            if u >= third and at < blocks:
+                stop = blocks if u == units - 1 else min(at + SHARE, blocks)
+                invert(at, stop)
+                at = stop
+        basis()
         for c in range(count):
-            if c + lag < count:
-                near(c + lag)
-            if c == min(3, count - 1):
-                gram_third()
-            if "a" in state and state["at"] < blocks:
-                invert(-(-blocks // min(4, count)) if c < count - 1 else blocks)
-                if state["at"] == blocks and "inverse" not in state:
-                    state["inverse"] = lower(state["a"])
-                    basis()
-            far(c)
-            if "inverse" in state:
-                while done <= c:
-                    correct(done)
-                    done += 1
+            correct(c)
+
+    @pl.when(jnp.logical_not(outer))
+    def _():
+        with jax.named_scope("q4_gram3"):
+            work[...] = gram_whole(1, last)
+        invert(0, blocks)
+        basis()
+        for u in range(units):
+            with jax.named_scope(f"q3_end{u}"):
+                far(u)
+            if (u + 1) % parts == 0:
+                correct(u // parts)
+
     with jax.named_scope("q8_squares"):
-        squares[me] = jnp.broadcast_to(state["squares"], (8, rank))
         copies = []
         for k in range(1, plane):
             copy = remote(squares.at[me], squares.at[me], square_send.at[k - 1], square_recv.at[k - 1], peer(k)[1])
@@ -449,13 +485,13 @@
         mean = summed(squares, plane)[:1] / (cols * plane)
         following_ref[...] = right_ref[...] / jnp.sqrt(mean + epsilon)
         if depth > 1:
-            for c in range(count):
-                inward(c).wait_send()
+            for u in range(units):
+                inward(u).wait_send()
 
             @pl.when(outer)
             def _():
-                for c in range(count):
-                    outward(c).wait_send()
+                for u in range(units):
+                    outward(u).wait_send()
 
 
 def finish(scale, mixed_ref, pair_ref, following_ref, next_ref, direction_ref, out_ref, direction_vmem, sems):
@@ -513,6 +549,7 @@
             pltpu.VMEM((rows, cols), bf16),
             pltpu.VMEM((rows, cols), bf16),
             pltpu.VMEM((cols, rank), f32),
+            pltpu.VMEM((cols, 2 * rank), bf16),
             pltpu.VMEM((rows, rank), f32),
             pltpu.VMEM((chips, own, rank), f32),
             pltpu.VMEM((others, own, rank), f32),
@@ -527,6 +564,7 @@
             pltpu.VMEM((2, z, rank // plane, rank), f32),
             pltpu.VMEM((2, plane, rank // plane, rank), f32),
             pltpu.VMEM((plane, 8, rank), f32),
+            pltpu.VMEM((rank, rank), f32),
             dma((2, plane)),
             dma,
             dma((chips,)),
@@ -538,8 +576,8 @@
             dma((2,)),
             dma((2, 3, most)),
             dma((2, 3, most)),
-            dma((2, count)),
-            dma((2, count)),
+            dma((2, 2 * count)),
+            dma((2, 2 * count)),
             dma((most,)),
             dma((most,)),
         ],

time: 72 us -> 66.3 us (0.921)
  Pallas kernels: 71.2 us -> 65.4 us
    pallas_call x1, Pallas kernels: 66.3 us -> 60.4 us  [shards(): pl.pallas_call(functools.partial(factors, shape), out_shape=[pltpu.VMEM((...]
where the time goes in v3:
time: 66.3 us; the launch traced here: 66.2 us
  Pallas kernels  65.4 us (99%)
  between operations  0.8 us (1%)
    pallas_call x1, Pallas kernels, shards(): pl.pallas_call(functools.partial(factors, shape), out_shape=[pltpu.VMEM((...  60.4 us
    pallas_call x1, Pallas kernels, shards(): pl.pallas_call(functools.partial(finish, scale), out_shape=[jax.ShapeDtyp...  4.92 us

profile of v3, /device:TPU:0, one launch (start us, length us, event | category | flops | bytes accessed | tf_op | source)
XLA Modules:
  0.0 66.2 jit_solution(10947781472927675017)
XLA Ops:
  0.6 60.4 %factors.1 = (f32[2048,1024]{1,0:T(8,128)S(1)}, bf16[2048,256]{1,0:T(8,128)(2,1)S(1)}, f32[1024,128]{1,0:T(8,128)}, f32[1024,128]{1,0:T(8,128)S(1)}) custom-call(f32[2048,1024]{1,0:T(8,128)} %bitcast.6, bf16[2048,1024]{1,0:T(8,128)(2,1)} %bitcast.7, f32[1024,128]{1,0:T(8,128)} %bitcast.8), custom_call_target="tpu_custom_call" | custom-call | tf_op jit(solution)/shard_map/factors/pallas_call | solution.py:537
  61.1 4.9 %finish.1 = (f32[2048,1024]{1,0:T(8,128)}, bf16[2048,1024]{1,0:T(8,128)(2,1)}, f32[1024,128]{1,0:T(8,128)}) custom-call(f32[2048,1024]{1,0:T(8,128)S(1)} %get-tuple-element.9.mixed_ref, bf16[2048,256]{1,0:T(8,128)(2,1)S(1)} %get-tuple-element.10.pair_ref, f32[1024,128]{1,0:T(8,128)S(1)} %get-tuple-element.11.following_ref), custom_call_target="tpu_custom_call" | custom-call | tf_op jit(solution)/shard_map/finish/pallas_call | solution.py:591

commit v4 on v3

--- a/solution.py
+++ b/solution.py
@@ -97,9 +97,8 @@
 
 def factors(shape, momentum_ref, gradient_ref, prior_ref, mixed, pair_ref, right_ref, following_ref,
             raw, wide_high, wide_low, prior_vmem, prior_pair, left, core_in, plane_in, whole, turned, value_t, sums, totals,
-            arrive, pieces, piece_in, piece_z, piece_all, squares, work, load_sem, prior_sem, core_send, core_recv,
-            plane_send, plane_recv, ag_send, ag_recv, half_sem, gram_send, gram_recv, chain_send, chain_recv,
-            square_send, square_recv):
+            arrive, pieces, piece_in, piece_z, piece_all, squares, work, load_sem, prior_sem, core_recv, once,
+            gram_send, gram_recv, chain_send, chain_recv):
     rows, cols = mixed.shape
     rank = prior_ref.shape[1]
     depth, dp = shape["shard"], shape["dp"]
@@ -132,8 +131,8 @@
 
     def load(slot, at):
         return (
-            pltpu.make_async_copy(momentum_ref.at[at], mixed.at[at], load_sem.at[0, slot]),
-            pltpu.make_async_copy(gradient_ref.at[at], raw.at[at], load_sem.at[1, slot]),
+            pltpu.make_async_copy(momentum_ref.at[at], mixed.at[at], load_sem.at[0, lax.rem(slot, AHEAD)]),
+            pltpu.make_async_copy(gradient_ref.at[at], raw.at[at], load_sem.at[1, lax.rem(slot, AHEAD)]),
         )
 
     loads = chips * cores
@@ -190,12 +189,15 @@
 
     def core_copy(i):
         at = place(cores - 1 - core, chip(chips - 1 - i)[0])
-        return remote(left.at[at], core_in.at[i], core_send.at[i], core_recv.at[i], partner)
+        return remote(left.at[at], core_in.at[i], once.at[0], core_recv.at[i], partner)
 
     def plane_copy(offset):
         index, device = chip(offset)
         slot = offset - 1
-        return remote(left.at[place(core, index)], plane_in.at[slot], plane_send.at[slot], plane_recv.at[slot], device)
+        return remote(left.at[place(core, index)], plane_in.at[slot], once.at[1], once.at[2], device)
+
+    def bulk(first):
+        return remote(plane_in, plane_in, once.at[first], once.at[first + 1], chip(1)[1])
 
     def settle(i):
         offset = chips - 1 - i
@@ -228,8 +230,9 @@
     with jax.named_scope("p3_rswait"):
         settle(chips - 1)
         total = left[mine, :]
+        if chips > 1:
+            bulk(1).wait_recv()
         for offset in range(1, chips):
-            plane_copy(offset).wait_recv()
             total = total + plane_in[offset - 1]
         whole[mine, :] = total
 
@@ -242,64 +245,56 @@
         return value
 
     def gram_sends(turn, stage, n, find, source, target):
-        copies = []
         for k in range(1, n):
             other, device = find(k)
-            copy = remote(source(other), target, gram_send.at[turn, stage, k - 1],
-                          gram_recv.at[turn, stage, k - 1], device)
-            copy.start()
-            copies.append(copy)
-        return copies
+            remote(source(other), target, gram_send.at[turn, stage], gram_recv.at[turn, stage], device).start()
+
+    def gram_wait(turn, stage, n, find, slots):
+        if n > 1:
+            part = slots.at[turn, pl.ds(0, n - 1)]
+            remote(part, part, gram_send.at[turn, stage], gram_recv.at[turn, stage], find(1)[1]).wait()
 
     def gram_steps(turn, gram):
         for i in range(plane):
             pieces[turn, i] = gram[i * piece : (i + 1) * piece]
         piece_in[turn, me] = pieces[turn, me]
-        copies = gram_sends(turn, 0, plane, peer, lambda i: pieces.at[turn, i], piece_in.at[turn, me])
+        gram_sends(turn, 0, plane, peer, lambda i: pieces.at[turn, i], piece_in.at[turn, me])
         yield
-        for copy in copies:
-            copy.wait()
+        gram_wait(turn, 0, plane, peer, piece_in)
         piece_z[turn, s] = summed(piece_in.at[turn], plane)
         mine_z = piece_z.at[turn, s]
-        copies = gram_sends(turn, 1, depth, across, lambda i: mine_z, mine_z)
+        gram_sends(turn, 1, depth, across, lambda i: mine_z, mine_z)
         yield
-        for copy in copies:
-            copy.wait()
+        gram_wait(turn, 1, depth, across, piece_z)
         piece_all[turn, me] = summed(piece_z.at[turn], depth)
         mine_all = piece_all.at[turn, me]
-        copies = gram_sends(turn, 2, plane, peer, lambda i: mine_all, mine_all)
-        yield copies
-
-    def gram_whole(turn, copies):
-        for copy in copies:
-            copy.wait()
+        gram_sends(turn, 2, plane, peer, lambda i: mine_all, mine_all)
+        yield
+
+    def gram_whole(turn):
+        gram_wait(turn, 2, plane, peer, piece_all)
         return jnp.concatenate([piece_all[turn, i] for i in range(plane)], axis=0)
 
     with jax.named_scope("p4_gram"):
         steps = gram_steps(0, dot(total, total, ROWS, HIGHEST))
         next(steps)
-    spread = []
     for offset in range(1, chips):
-        copy = remote(whole.at[mine], whole.at[mine], ag_send.at[offset - 1], ag_recv.at[offset - 1], chip(offset)[1])
-        copy.start()
-        spread.append(copy)
+        remote(whole.at[mine], whole.at[mine], once.at[3], once.at[4], chip(offset)[1]).start()
     with jax.named_scope("p5_gram1"):
         next(steps)
     with jax.named_scope("p6_gram2"):
-        last = next(steps)
+        next(steps)
     with jax.named_scope("p7_agwait"):
-        for offset in range(1, chips):
-            plane_copy(offset).wait_send()
-        for copy in spread:
-            copy.wait()
+        if chips > 1:
+            bulk(1).wait_send()
+            bulk(3).wait()
         if cores == 2:
-            for i in range(chips):
-                core_copy(i).wait_send()
             at = pl.ds(pl.multiple_of(core * (rows // 2), 8), rows // 2)
-            half_copy = remote(whole.at[at], whole.at[at], half_sem.at[0], half_sem.at[1], partner)
+            remote(left.at[at], left.at[at], once.at[0], once.at[0], partner).wait_send()
+            half_copy = remote(whole.at[at], whole.at[at], once.at[5], once.at[6], partner)
             half_copy.start()
     with jax.named_scope("p8_gram3"):
-        gram = gram_whole(0, last)
+        gram = gram_whole(0)
     with jax.named_scope("p9_inv1"):
         inverse = lower(inverse_steps(gram, 0, rank // 8))
     with jax.named_scope("q0_value"):
@@ -340,15 +335,15 @@
 
     def inward(u):
         slot = jnp.where(middle, 1, 0)
-        return remote(unit(sums, u), unit(arrive.at[slot], u), chain_send.at[0, u], chain_recv.at[slot, u],
+        return remote(unit(sums, u), unit(arrive.at[slot], u), chain_send.at[0], chain_recv.at[slot, u],
                       {"shard": s + step_in})
 
     def outward(u):
-        return remote(unit(totals, u), unit(arrive.at[1], u), chain_send.at[1, u], chain_recv.at[1, u],
+        return remote(unit(totals, u), unit(arrive.at[1], u), chain_send.at[1], chain_recv.at[1, u],
                       {"shard": s - step_in})
 
     def landed(slot, u):
-        remote(unit(sums, u), unit(arrive.at[slot], u), chain_send.at[0, u], chain_recv.at[slot, u],
+        remote(unit(sums, u), unit(arrive.at[slot], u), chain_send.at[0], chain_recv.at[slot, u],
                {"shard": s + step_in}).wait_recv()
 
     def near(u):
@@ -392,11 +387,10 @@
                         inward(u).start()
 
     lag = min(LAG, units)
-    last = None
     for u in range(lag):
         if u == max(lag - 2, 0):
             with jax.named_scope("q4_gram2"):
-                last = next(steps)
+                next(steps)
         with jax.named_scope("q3_near"):
             near(u)
 
@@ -442,7 +436,7 @@
                     near(u + lag)
             if u == third:
                 with jax.named_scope("q4_gram3"):
-                    work[...] = gram_whole(1, last)
+                    work[...] = gram_whole(1)
             if u >= third and at < blocks:
                 stop = blocks if u == units - 1 else min(at + SHARE, blocks)
                 invert(at, stop)
@@ -454,7 +448,7 @@
     @pl.when(jnp.logical_not(outer))
     def _():
         with jax.named_scope("q4_gram3"):
-            work[...] = gram_whole(1, last)
+            work[...] = gram_whole(1)
         invert(0, blocks)
         basis()
         for u in range(units):
@@ -464,11 +458,8 @@
                 correct(u // parts)
 
     with jax.named_scope("q8_squares"):
-        copies = []
         for k in range(1, plane):
-            copy = remote(squares.at[me], squares.at[me], square_send.at[k - 1], square_recv.at[k - 1], peer(k)[1])
-            copy.start()
-            copies.append(copy)
+            remote(squares.at[me], squares.at[me], once.at[7], once.at[8], peer(k)[1]).start()
     with jax.named_scope("q9_momentum"):
         scaled = (right_ref[...] * (decay_rate - 1.0)).astype(jnp.bfloat16)
 
@@ -480,29 +471,28 @@
 
         lax.fori_loop(0, STEPS, update, 0)
     with jax.named_scope("r0_follow"):
-        for copy in copies:
-            copy.wait()
+        if plane > 1:
+            part = squares.at[pl.ds(0, plane - 1)]
+            remote(part, part, once.at[7], once.at[8], peer(1)[1]).wait()
         mean = summed(squares, plane)[:1] / (cols * plane)
         following_ref[...] = right_ref[...] / jnp.sqrt(mean + epsilon)
         if depth > 1:
-            for u in range(units):
-                inward(u).wait_send()
+            remote(sums, sums, chain_send.at[0], chain_recv.at[0, 0], {"shard": s + step_in}).wait_send()
 
             @pl.when(outer)
             def _():
-                for u in range(units):
-                    outward(u).wait_send()
+                remote(totals, totals, chain_send.at[1], chain_recv.at[0, 0], {"shard": s - step_in}).wait_send()
 
 
 def finish(scale, mixed_ref, pair_ref, following_ref, next_ref, direction_ref, out_ref, direction_vmem, sems):
     rows = mixed_ref.shape[0]
     rank = following_ref.shape[1]
     block = rows // STEPS
-    copies = [pltpu.make_async_copy(following_ref, out_ref, sems.at[2, 0])]
-    for i in range(STEPS):
-        at = pl.ds(i * block, block)
-        copies.append(pltpu.make_async_copy(mixed_ref.at[at], next_ref.at[at], sems.at[0, i]))
-    for copy in copies:
+    moves = (
+        pltpu.make_async_copy(mixed_ref, next_ref, sems.at[0]),
+        pltpu.make_async_copy(following_ref, out_ref, sems.at[1]),
+    )
+    for copy in moves:
         copy.start()
     high, low = split(following_ref[...] * scale)
     follow = jnp.concatenate([high, high], axis=1)
@@ -510,11 +500,10 @@
         at = pl.ds(i * block, block)
         value = dot(pair_ref[at, :], follow, TURNED) + dot(pair_ref[at, :rank], low, TURNED)
         direction_vmem[at, :] = value.astype(jnp.bfloat16)
-        copy = pltpu.make_async_copy(direction_vmem.at[at], direction_ref.at[at], sems.at[1, i])
-        copy.start()
-        copies.append(copy)
-    for copy in copies:
+        pltpu.make_async_copy(direction_vmem.at[at], direction_ref.at[at], sems.at[2]).start()
+    for copy in moves:
         copy.wait()
+    pltpu.make_async_copy(direction_vmem, direction_ref, sems.at[2]).wait()
 
 
 def shards(shape, gradient, momentum, prior_right_factor):
@@ -533,7 +522,6 @@
     hbm = pl.BlockSpec(memory_space=pltpu.HBM)
     f32, bf16 = jnp.float32, jnp.bfloat16
     others = max(chips - 1, 1)
-    most = max(plane, z)
     mixed, pair, right, following = pl.pallas_call(
         functools.partial(factors, shape),
         out_shape=[
@@ -565,21 +553,14 @@
             pltpu.VMEM((2, plane, rank // plane, rank), f32),
             pltpu.VMEM((plane, 8, rank), f32),
             pltpu.VMEM((rank, rank), f32),
-            dma((2, plane)),
+            dma((2, AHEAD)),
             dma,
             dma((chips,)),
-            dma((chips,)),
-            dma((others,)),
-            dma((others,)),
-            dma((others,)),
-            dma((others,)),
+            dma((9,)),
+            dma((2, 3)),
+            dma((2, 3)),
             dma((2,)),
-            dma((2, 3, most)),
-            dma((2, 3, most)),
             dma((2, 2 * count)),
-            dma((2, 2 * count)),
-            dma((most,)),
-            dma((most,)),
         ],
         compiler_params=pltpu.CompilerParams(
             collective_id=0, has_side_effects=True, vmem_limit_bytes=36 * MiB
@@ -597,7 +578,7 @@
         ],
         in_specs=[vmem, vmem, vmem],
         out_specs=[hbm, hbm, hbm],
-        scratch_shapes=[pltpu.VMEM((rows, cols), bf16), dma((3, STEPS))],
+        scratch_shapes=[pltpu.VMEM((rows, cols), bf16), dma((3,))],
         compiler_params=pltpu.CompilerParams(vmem_limit_bytes=24 * MiB),
         name="finish",
     )(mixed, pair, following)

time: 66.3 us -> 64.8 us (0.977)
  Pallas kernels: 65.4 us -> 63.8 us
    pallas_call x1, Pallas kernels: 60.4 us -> 59 us  [shards(): pl.pallas_call(functools.partial(factors, shape), out_shape=[pltpu.VMEM((...]
where the time goes in v4:
time: 64.8 us; the launch traced here: 64.6 us
  Pallas kernels  63.8 us (98%)
  between operations  0.8 us (1%)
    pallas_call x1, Pallas kernels, shards(): pl.pallas_call(functools.partial(factors, shape), out_shape=[pltpu.VMEM((...  59 us
    pallas_call x1, Pallas kernels, shards(): pl.pallas_call(functools.partial(finish, scale), out_shape=[jax.ShapeDtyp...  4.84 us

profile of v4, /device:TPU:0, one launch (start us, length us, event | category | flops | bytes accessed | tf_op | source)
XLA Modules:
  0.0 64.6 jit_solution(13797366862415146607)
XLA Ops:
  0.6 59.0 %factors.1 = (f32[2048,1024]{1,0:T(8,128)S(1)}, bf16[2048,256]{1,0:T(8,128)(2,1)S(1)}, f32[1024,128]{1,0:T(8,128)}, f32[1024,128]{1,0:T(8,128)S(1)}) custom-call(f32[2048,1024]{1,0:T(8,128)} %bitcast.6, bf16[2048,1024]{1,0:T(8,128)(2,1)} %bitcast.7, f32[1024,128]{1,0:T(8,128)} %bitcast.8), custom_call_target="tpu_custom_call" | custom-call | tf_op jit(solution)/shard_map/factors/pallas_call | solution.py:525
  59.6 4.8 %finish.1 = (f32[2048,1024]{1,0:T(8,128)}, bf16[2048,1024]{1,0:T(8,128)(2,1)}, f32[1024,128]{1,0:T(8,128)}) custom-call(f32[2048,1024]{1,0:T(8,128)S(1)} %get-tuple-element.9.mixed_ref, bf16[2048,256]{1,0:T(8,128)(2,1)S(1)} %get-tuple-element.10.pair_ref, f32[1024,128]{1,0:T(8,128)S(1)} %get-tuple-element.11.following_ref), custom_call_target="tpu_custom_call" | custom-call | tf_op jit(solution)/shard_map/finish/pallas_call | solution.py:572

commit v5 on v4

--- a/solution.py
+++ b/solution.py
@@ -13,9 +13,10 @@
 epsilon = 1e-06
 STEPS = 8
 AHEAD = 3
-LAG = 5
-THIRD = 4
-SHARE = 1
+GAP = 5.3
+THIRD = 12
+SHARE = 2
+MOVES = (1, 1, 1, 2, 2, 3)
 MiB = 1024 * 1024
 ROWS, NORMAL, TURNED = ((0,), (0,)), ((1,), (0,)), ((1,), (1,))
 
@@ -77,8 +78,69 @@
     return lax.fori_loop(start, stop, block, a)
 
 
-def lower(a):
-    rows = lax.broadcasted_iota(jnp.int32, a.shape, 0)
+def unit_diagonal(gram):
+    rows = lax.broadcasted_iota(jnp.int32, gram.shape, 0)
+    lanes = lax.broadcasted_iota(jnp.int32, gram.shape, 1)
+    diagonal = jnp.where(rows == lanes, gram, 0.0)
+    across = lax.rsqrt(jnp.sum(diagonal, axis=0, keepdims=True))
+    down = lax.rsqrt(jnp.sum(diagonal, axis=1, keepdims=True))
+    return gram * across * down, across
+
+def eliminate(blocks, k):
+    size = blocks[0].shape[1]
+    sub = lax.broadcasted_iota(jnp.int32, (8, size), 0)
+    lane = lax.broadcasted_iota(jnp.int32, (8, size), 1) - 8 * k
+    here = (lane >= 0) & (lane < 8)
+
+    def row(value, index):
+        return jnp.broadcast_to(value[index : index + 1], value.shape)
+
+    def column(value, index):
+        return jnp.broadcast_to(value[:, 8 * k + index : 8 * k + index + 1], value.shape)
+
+    top = blocks[k]
+    columns = [column(top, c) for c in range(8)]
+    e = {(i, j): row(columns[j], i) for j in range(8) for i in range(j, 8)}
+    panel = jnp.where(here, jnp.where(lane == sub, 1.0, 0.0), top)
+    x = [row(panel, i) for i in range(8)]
+    y, z, f = [None] * 8, [None] * 8, {}
+    for p in range(0, 8, 2):
+        a, b, c = e[p, p], e[p + 1, p], e[p + 1, p + 1]
+        root = lax.rsqrt(a * c - b * b)
+        inverse = root * root
+        g = {}
+        for i in range(p + 2, 8):
+            g[i] = (e[i, p] * c - e[i, p + 1] * b, e[i, p + 1] * a - e[i, p] * b)
+        for i in range(p + 2, 8):
+            for j in range(p + 2, i + 1):
+                e[i, j] = e[i, j] - (g[i][0] * e[j, p] + g[i][1] * e[j, p + 1]) * inverse
+        for i in range(p + 2, 8):
+            f[i, p], f[i, p + 1] = g[i][0] * inverse, g[i][1] * inverse
+            x[i] = x[i] - (f[i, p] * x[p] + f[i, p + 1] * x[p + 1])
+        first = lax.rsqrt(a)
+        y[p] = x[p] * first
+        y[p + 1] = (x[p + 1] * a - b * x[p]) * (first * root)
+        z[p] = (c * x[p] - b * x[p + 1]) * inverse
+        z[p + 1] = (a * x[p + 1] - b * x[p]) * inverse
+    for p in (4, 2, 0):
+        for i in range(p + 2, 8):
+            z[p] = z[p] - f[i, p] * z[i]
+            z[p + 1] = z[p + 1] - f[i, p + 1] * z[i]
+    done = y[0]
+    for i in range(1, 8):
+        done = jnp.where(sub == i, y[i], done)
+    out = list(blocks)
+    out[k] = done
+    for r in range(k + 1, len(blocks)):
+        rest = jnp.where(here, 0.0, blocks[r])
+        for c in range(8):
+            rest = rest - column(blocks[r], c) * z[c]
+        out[r] = rest
+    return out
+
+
+def lower(a, start=0):
+    rows = lax.broadcasted_iota(jnp.int32, a.shape, 0) + start
     lanes = lax.broadcasted_iota(jnp.int32, a.shape, 1)
     return jnp.where(rows >= lanes, a, 0.0)
 
@@ -96,7 +158,7 @@
 
 
 def factors(shape, momentum_ref, gradient_ref, prior_ref, mixed, pair_ref, right_ref, following_ref,
-            raw, wide_high, wide_low, prior_vmem, prior_pair, left, core_in, plane_in, whole, turned, value_t, sums, totals,
+            raw, wide_high, wide_low, prior_vmem, prior_pair, left, core_in, plane_in, whole, fine, turned, sums, totals,
             arrive, pieces, piece_in, piece_z, piece_all, squares, work, load_sem, prior_sem, core_recv, once,
             gram_send, gram_recv, chain_send, chain_recv):
     rows, cols = mixed.shape
@@ -254,36 +316,36 @@
             part = slots.at[turn, pl.ds(0, n - 1)]
             remote(part, part, gram_send.at[turn, stage], gram_recv.at[turn, stage], find(1)[1]).wait()
 
-    def gram_steps(turn, gram):
+    def gram_start(turn, gram):
         for i in range(plane):
             pieces[turn, i] = gram[i * piece : (i + 1) * piece]
         piece_in[turn, me] = pieces[turn, me]
         gram_sends(turn, 0, plane, peer, lambda i: pieces.at[turn, i], piece_in.at[turn, me])
-        yield
+
+    def gram_across(turn):
         gram_wait(turn, 0, plane, peer, piece_in)
         piece_z[turn, s] = summed(piece_in.at[turn], plane)
         mine_z = piece_z.at[turn, s]
         gram_sends(turn, 1, depth, across, lambda i: mine_z, mine_z)
-        yield
+
+    def gram_spread(turn):
         gram_wait(turn, 1, depth, across, piece_z)
         piece_all[turn, me] = summed(piece_z.at[turn], depth)
         mine_all = piece_all.at[turn, me]
         gram_sends(turn, 2, plane, peer, lambda i: mine_all, mine_all)
-        yield
 
     def gram_whole(turn):
         gram_wait(turn, 2, plane, peer, piece_all)
         return jnp.concatenate([piece_all[turn, i] for i in range(plane)], axis=0)
 
     with jax.named_scope("p4_gram"):
-        steps = gram_steps(0, dot(total, total, ROWS, HIGHEST))
-        next(steps)
+        gram_start(0, dot(total, total, ROWS, HIGHEST))
     for offset in range(1, chips):
         remote(whole.at[mine], whole.at[mine], once.at[3], once.at[4], chip(offset)[1]).start()
     with jax.named_scope("p5_gram1"):
-        next(steps)
+        gram_across(0)
     with jax.named_scope("p6_gram2"):
-        next(steps)
+        gram_spread(0)
     with jax.named_scope("p7_agwait"):
         if chips > 1:
             bulk(1).wait_send()
@@ -295,43 +357,15 @@
             half_copy.start()
     with jax.named_scope("p8_gram3"):
         gram = gram_whole(0)
-    with jax.named_scope("p9_inv1"):
-        inverse = lower(inverse_steps(gram, 0, rank // 8))
-    with jax.named_scope("q0_value"):
-        if cores == 2:
-            half_copy.wait()
-        w_high, w_middle, w_low = split3(inverse)
-        ends = jnp.concatenate(
-            [jnp.concatenate([w_high, w_middle], axis=1), jnp.concatenate([w_middle, w_high], axis=1)], axis=0
-        )
-        tail = jnp.concatenate([w_low, w_high], axis=1)
-        for i in range(STEPS):
-            block = rows // STEPS
-            at = slice(i * block, (i + 1) * block)
-            high, middle_part, low = split3(whole[at, :])
-            both = dot(ends, jnp.concatenate([high, middle_part], axis=1), TURNED)
-            value = both[:rank] + (both[rank:] + dot(tail, jnp.concatenate([high, low], axis=1), TURNED))
-            value_t[:, at] = value
-            high, low = split(value)
-            turned[:rank, at] = high
-            turned[rank:, at] = low
-    with jax.named_scope("q1_gram"):
-        begin = pl.multiple_of((core * chips + x * dp + y) * own, 128 if own % 128 == 0 else 8)
-        if own % 128 == 0:
-            part = value_t[:, pl.ds(begin, own)]
-            gram = dot(part, part, TURNED, HIGHEST)
-        else:
-            part = dot(whole[mine, :], inverse, TURNED, HIGHEST)
-            gram = dot(part, part, ROWS, HIGHEST)
-        steps = gram_steps(1, gram)
-        next(steps)
-
     parts = 2 if rank % 16 == 0 else 1
     tall = rank // parts
     units = count * parts
+    blocks = rank // 8
+    per = group // chunk
+    groups = cols // group
 
     def unit(ref, u):
-        return ref.at[u // parts, pl.ds((u % parts) * tall, tall)]
+        return ref.at[u % count, pl.ds((u // count) * tall, tall)]
 
     def inward(u):
         slot = jnp.where(middle, 1, 0)
@@ -347,78 +381,149 @@
                {"shard": s + step_in}).wait_recv()
 
     def near(u):
-        if depth > 1:
-
-            @pl.when(outer)
-            def _():
-                landed(0, u)
-                unit(sums, u)[...] = unit(sums, u)[...] + unit(arrive.at[0], u)[...]
-                inward(u).start()
-
-    def far(u):
+        landed(0, u)
+        unit(sums, u)[...] = unit(sums, u)[...] + unit(arrive.at[0], u)[...]
+        inward(u).start()
+
+    def far(u, forward):
         if depth > 1:
             landed(1, u)
             got = unit(arrive.at[1], u)[...]
             unit(totals, u)[...] = jnp.where(middle, unit(sums, u)[...] + got, got)
-
-            @pl.when(outer)
-            def _():
+            if forward:
                 outward(u).start()
         else:
             unit(totals, u)[...] = unit(sums, u)[...]
 
-    per = group // chunk
-    groups = cols // group
-    with jax.named_scope("q2_right"):
+    def due(step, u):
+        late = 0.0 if u < count else 1.7 if 2 * u < 3 * count else 2.4
+        return u + late + (GAP if step is far else 0.0)
+
+    queue = sorted(((step, u) for u in range(units) for step in (near, far)), key=lambda item: due(*item))
+
+    def take(n, computed):
+        steps = []
+        while len(steps) < n and len(queue) > 1 and queue[0][1] < computed:
+            steps.append(queue.pop(0))
+        if depth > 2 and steps:
+
+            @pl.when(outer)
+            def _():
+                for step, u in steps:
+                    with jax.named_scope(f"q3_{step.__name__}{u}"):
+                        step(u, True) if step is far else step(u)
+
+    def basis_half(r, w):
+        for i in range(STEPS):
+            block = rows // STEPS
+            at = slice(i * block, (i + 1) * block)
+            if r == 0:
+                high, middle_part, low = split3(whole[at, :])
+                fine[0, at, :rank] = high
+                fine[0, at, rank:] = middle_part
+                fine[1, at, :rank] = high
+                fine[1, at, rank:] = low
+            value = value_of(w, fine[0, at, :], fine[1, at, :])
+            high, low = split(value)
+            turned[r, :tall, at] = high
+            turned[r, tall:, at] = low
+
+    def value_of(w, block, tail_block):
+        w_high, w_middle, w_low = split3(w)
+        ends = jnp.concatenate(
+            [jnp.concatenate([w_high, w_middle], axis=1), jnp.concatenate([w_middle, w_high], axis=1)], axis=0
+        )
+        both = dot(ends, block, TURNED)
+        return both[:tall] + (both[tall:] + dot(jnp.concatenate([w_low, w_high], axis=1), tail_block, TURNED))
+
+    def right_group(r, g):
+        at = slice(g * group, (g + 1) * group)
+        both = dot(turned[r], wide_high[:, at], NORMAL)
+        value = both[:tall] + both[tall:] + dot(turned[r, :tall, :], wide_low[:, at], NORMAL)
+        for i in range(per):
+            sums[g * per + i, r * tall : (r + 1) * tall, :] = value[:, i * chunk : (i + 1) * chunk]
+
+    def right_send(r, g):
+        if depth > 1:
+
+            @pl.when(jnp.logical_not(outer))
+            def _():
+                for i in range(per):
+                    inward(r * count + g * per + i).start()
+
+    with jax.named_scope("p9_inv1"):
+        scaled, lanes = unit_diagonal(gram)
+        rest = [scaled[8 * i : 8 * i + 8] for i in range(blocks)]
+        weights = []
+    for r in range(parts):
+        with jax.named_scope(f"p9_half{r}"):
+            first_block, stop = r * blocks // parts, (r + 1) * blocks // parts
+            for k in range(first_block, stop):
+                rest = eliminate(rest, k)
+                if r > 0 and k == first_block + 5:
+                    take(1, r * count)
+            weights.append(lower(jnp.concatenate(rest[first_block:stop], axis=0), 8 * first_block) * lanes)
+        last_part = r == parts - 1
+        if last_part:
+            take(1, r * count)
+            with jax.named_scope("q1_gram"):
+                if r == 0 and cores == 2:
+                    half_copy.wait()
+                high, middle_part, low = split3(whole[mine, :])
+                block = jnp.concatenate([high, middle_part], axis=1)
+                tail_block = jnp.concatenate([high, low], axis=1)
+                part = jnp.concatenate([value_of(w, block, tail_block) for w in weights], axis=0)
+                gram_start(1, dot(part, part, TURNED, HIGHEST))
+            take(MOVES[0], r * count)
+        with jax.named_scope(f"q0_value{r}"):
+            if cores == 2 and r == 0 and not last_part:
+                half_copy.wait()
+            basis_half(r, weights[r])
+        if last_part:
+            take(MOVES[1], r * count)
         for g in range(groups):
-            at = slice(g * group, (g + 1) * group)
-            both = dot(turned[...], wide_high[:, at], NORMAL)
-            value = both[:rank] + both[rank:] + dot(turned[:rank], wide_low[:, at], NORMAL)
-            for i in range(per):
-                sums[g * per + i] = value[:, i * chunk : (i + 1) * chunk]
-            if g == min(1, groups - 1):
+            with jax.named_scope(f"q2_right{r}{g}"):
+                right_group(r, g)
+            if last_part and g == min(2, groups - 1):
                 with jax.named_scope("q2_gram1"):
-                    next(steps)
-            if depth > 1:
-
-                @pl.when(jnp.logical_not(outer))
-                def _():
-                    for u in range(g * per * parts, (g + 1) * per * parts):
-                        inward(u).start()
-
-    lag = min(LAG, units)
-    for u in range(lag):
-        if u == max(lag - 2, 0):
-            with jax.named_scope("q4_gram2"):
-                next(steps)
-        with jax.named_scope("q3_near"):
-            near(u)
-
-    blocks = rank // 8
-
-    def invert(start, stop):
+                    gram_across(1)
+            right_send(r, g)
+            if last_part:
+                take(MOVES[2 + min(g, 3)], r * count + (g + 1) * per)
+
+    def second():
+        with jax.named_scope("q4_gram3"):
+            scaled, across_lanes = unit_diagonal(gram_whole(1))
+        return [scaled[8 * i : 8 * i + 8] for i in range(blocks)], across_lanes
+
+    def invert(rest, start, stop):
         with jax.named_scope("q5_inv2"):
-            work[...] = inverse_steps(work[...], start, stop)
+            for k in range(start, stop):
+                rest = eliminate(rest, k)
+        return rest
+
+    def keep(rest, across_lanes):
+        work[...] = lower(jnp.concatenate(rest, axis=0)) * across_lanes
 
     def basis():
         with jax.named_scope("q6_basis"):
-            work[...] = lower(work[...])
             high, low = split(work[...])
-            left_pair = jnp.concatenate([high, low], axis=1)
+            pair = jnp.concatenate([high, low], axis=1)
             for i in range(STEPS):
                 block = rows // STEPS
                 at = slice(i * block, (i + 1) * block)
-                value = dot(
-                    left_pair, jnp.concatenate([turned[:rank, at], turned[:rank, at]], axis=0), NORMAL
-                ) + dot(high, turned[rank:, at], NORMAL)
+                top = jnp.concatenate([turned[r, :tall, at] for r in range(parts)], axis=0)
+                bottom = jnp.concatenate([turned[r, tall:, at] for r in range(parts)], axis=0)
+                value = dot(pair, jnp.concatenate([top, top], axis=0), NORMAL) + dot(high, bottom, NORMAL)
                 high_t, low_t = split(value.T)
                 pair_ref[at, :rank] = high_t
                 pair_ref[at, rank:] = low_t
 
-    def correct(c):
+    def correct(start, stop):
         with jax.named_scope("q7_right"):
-            value = dot(totals[c], work[...], ((0,), (1,)), HIGHEST)
-            right_ref[c * chunk : (c + 1) * chunk, :] = value
+            wide = jnp.concatenate([totals[c] for c in range(start, stop)], axis=1)
+            value = dot(wide, work[...], ((0,), (1,)), HIGHEST)
+            right_ref[start * chunk : stop * chunk, :] = value
             column = jnp.sum(value * value, axis=0, keepdims=True)
             squares[me] = squares[me] + jnp.broadcast_to(column, (8, rank))
 
@@ -426,40 +531,46 @@
 
     @pl.when(outer)
     def _():
-        third = min(THIRD, units - 1)
+        plan = list(queue)
+        second_at = next((i for i, (step, u) in enumerate(plan) if step is near and 2 * u >= 3 * count), 0)
+        third_at = next((i for i, (step, u) in enumerate(plan) if step is far and u >= THIRD), len(plan) - 1)
+        third_at = max(third_at, second_at)
         at = 0
-        for u in range(units):
-            with jax.named_scope("q3_far"):
-                far(u)
-            if u + lag < units:
-                with jax.named_scope("q3_near2"):
-                    near(u + lag)
-            if u == third:
-                with jax.named_scope("q4_gram3"):
-                    work[...] = gram_whole(1)
-            if u >= third and at < blocks:
-                stop = blocks if u == units - 1 else min(at + SHARE, blocks)
-                invert(at, stop)
+        for i, (step, u) in enumerate(plan):
+            if i == second_at:
+                with jax.named_scope("q4_gram2"):
+                    gram_spread(1)
+            with jax.named_scope(f"q3_{step.__name__}{u}"):
+                far(u, True) if step is far else near(u)
+            if i == third_at:
+                rest, across_lanes = second()
+            if i >= third_at and step is far:
+                stop = blocks if i == len(plan) - 1 else min(at + SHARE, blocks)
+                rest = invert(rest, at, stop)
                 at = stop
-        basis()
-        for c in range(count):
-            correct(c)
+        keep(rest, across_lanes)
+        for c in range(0, count, 2):
+            correct(c, min(c + 2, count))
 
     @pl.when(jnp.logical_not(outer))
     def _():
-        with jax.named_scope("q4_gram3"):
-            work[...] = gram_whole(1)
-        invert(0, blocks)
-        basis()
+        with jax.named_scope("q4_gram2"):
+            gram_spread(1)
+        rest, across_lanes = second()
+        keep(invert(rest, 0, blocks), across_lanes)
         for u in range(units):
             with jax.named_scope(f"q3_end{u}"):
-                far(u)
-            if (u + 1) % parts == 0:
-                correct(u // parts)
+                far(u, False)
+            if u == units - 1 - 2 * per:
+                for c in range(0, count - 2 * per, 2):
+                    correct(c, c + 2)
+        for c in range(max(count - 2 * per, 0) if count > 2 * per else 0, count, 2):
+            correct(c, min(c + 2, count))
 
     with jax.named_scope("q8_squares"):
         for k in range(1, plane):
             remote(squares.at[me], squares.at[me], once.at[7], once.at[8], peer(k)[1]).start()
+    basis()
     with jax.named_scope("q9_momentum"):
         scaled = (right_ref[...] * (decay_rate - 1.0)).astype(jnp.bfloat16)
 
@@ -517,6 +628,7 @@
     own = rows // plane
     group, chunk = widths(cols)
     count = cols // chunk
+    parts = 2 if rank % 16 == 0 else 1
     dma = pltpu.SemaphoreType.DMA
     vmem = pl.BlockSpec(memory_space=pltpu.VMEM)
     hbm = pl.BlockSpec(memory_space=pltpu.HBM)
@@ -542,8 +654,8 @@
             pltpu.VMEM((chips, own, rank), f32),
             pltpu.VMEM((others, own, rank), f32),
             pltpu.VMEM((rows, rank), f32),
-            pltpu.VMEM((2 * rank, rows), bf16),
-            pltpu.VMEM((rank, rows), f32),
+            pltpu.VMEM((2, rows, 2 * rank), bf16),
+            pltpu.VMEM((parts, 2 * rank // parts, rows), bf16),
             pltpu.VMEM((count, rank, chunk), f32),
             pltpu.VMEM((count, rank, chunk), f32),
             pltpu.VMEM((2, count, rank, chunk), f32),

time: 64.8 us -> 61.5 us (0.949)
  Pallas kernels: 63.8 us -> 60.6 us
    pallas_call x1, Pallas kernels: 59 us -> 55.7 us  [shards(): pl.pallas_call(functools.partial(factors, shape), out_shape=[pltpu.VMEM((...]
where the time goes in v5:
time: 61.5 us; the launch traced here: 61.4 us
  Pallas kernels  60.6 us (99%)
  between operations  0.8 us (1%)
    pallas_call x1, Pallas kernels, shards(): pl.pallas_call(functools.partial(factors, shape), out_shape=[pltpu.VMEM((...  55.7 us
    pallas_call x1, Pallas kernels, shards(): pl.pallas_call(functools.partial(finish, scale), out_shape=[jax.ShapeDtyp...  4.84 us

profile of v5, /device:TPU:0, one launch (start us, length us, event | category | flops | bytes accessed | tf_op | source)
XLA Modules:
  0.0 61.4 jit_solution(15964988775652768674)
XLA Ops:
  0.6 55.7 %factors.1 = (f32[2048,1024]{1,0:T(8,128)S(1)}, bf16[2048,256]{1,0:T(8,128)(2,1)S(1)}, f32[1024,128]{1,0:T(8,128)}, f32[1024,128]{1,0:T(8,128)S(1)}) custom-call(f32[2048,1024]{1,0:T(8,128)} %bitcast.6, bf16[2048,1024]{1,0:T(8,128)(2,1)} %bitcast.7, f32[1024,128]{1,0:T(8,128)} %bitcast.8), custom_call_target="tpu_custom_call" | custom-call | tf_op jit(solution)/shard_map/factors/pallas_call | solution.py:637
  56.4 4.8 %finish.1 = (f32[2048,1024]{1,0:T(8,128)}, bf16[2048,1024]{1,0:T(8,128)(2,1)}, f32[1024,128]{1,0:T(8,128)}) custom-call(f32[2048,1024]{1,0:T(8,128)S(1)} %get-tuple-element.9.mixed_ref, bf16[2048,256]{1,0:T(8,128)(2,1)S(1)} %get-tuple-element.10.pair_ref, f32[1024,128]{1,0:T(8,128)S(1)} %get-tuple-element.11.following_ref), custom_call_target="tpu_custom_call" | custom-call | tf_op jit(solution)/shard_map/finish/pallas_call | solution.py:684

commit v6 on v5

--- a/solution.py
+++ b/solution.py
@@ -157,8 +157,7 @@
     return group, chunk
 
 
-def factors(shape, momentum_ref, gradient_ref, prior_ref, mixed, pair_ref, right_ref, following_ref,
-            raw, wide_high, wide_low, prior_vmem, prior_pair, left, core_in, plane_in, whole, fine, turned, sums, totals,
+def factors(shape, momentum_ref, gradient_ref, prior_ref, mixed, pair_ref, following_ref, right_ref, raw, wide_high, wide_low, prior_vmem, prior_pair, left, core_in, plane_in, whole, fine, turned, sums, totals,
             arrive, pieces, piece_in, piece_z, piece_all, squares, work, load_sem, prior_sem, core_recv, once,
             gram_send, gram_recv, chain_send, chain_recv):
     rows, cols = mixed.shape
@@ -634,17 +633,17 @@
     hbm = pl.BlockSpec(memory_space=pltpu.HBM)
     f32, bf16 = jnp.float32, jnp.bfloat16
     others = max(chips - 1, 1)
-    mixed, pair, right, following = pl.pallas_call(
+    mixed, pair, following = pl.pallas_call(
         functools.partial(factors, shape),
         out_shape=[
             pltpu.VMEM((rows, cols), f32),
             pltpu.VMEM((rows, 2 * rank), bf16),
             pltpu.VMEM((cols, rank), f32),
-            pltpu.VMEM((cols, rank), f32),
         ],
         in_specs=[hbm, hbm, hbm],
-        out_specs=[vmem, vmem, vmem, vmem],
+        out_specs=[vmem, vmem, vmem],
         scratch_shapes=[
+            pltpu.VMEM((cols, rank), f32),
             pltpu.VMEM((rows, cols), bf16),
             pltpu.VMEM((rows, cols), bf16),
             pltpu.VMEM((rows, cols), bf16),

time: 61.5 us -> 60.7 us (0.987)
  Pallas kernels: 60.6 us -> 59.8 us
    pallas_call x1, Pallas kernels: 55.7 us -> 54.9 us  [shards(): pl.pallas_call(functools.partial(factors, shape), out_shape=[pltpu.VMEM((...]
where the time goes in v6:
time: 60.7 us; the launch traced here: 60.6 us
  Pallas kernels  59.8 us (99%)
  between operations  0.8 us (1%)
    pallas_call x1, Pallas kernels, shards(): pl.pallas_call(functools.partial(factors, shape), out_shape=[pltpu.VMEM((...  54.9 us
    pallas_call x1, Pallas kernels, shards(): pl.pallas_call(functools.partial(finish, scale), out_shape=[jax.ShapeDtyp...  4.84 us

profile of v6, /device:TPU:0, one launch (start us, length us, event | category | flops | bytes accessed | tf_op | source)
XLA Modules:
  0.0 60.6 jit_solution(5008513262978359397)
XLA Ops:
  0.6 54.9 %factors.1 = (f32[2048,1024]{1,0:T(8,128)S(1)}, bf16[2048,256]{1,0:T(8,128)(2,1)S(1)}, f32[1024,128]{1,0:T(8,128)S(1)}) custom-call(f32[2048,1024]{1,0:T(8,128)} %bitcast.6, bf16[2048,1024]{1,0:T(8,128)(2,1)} %bitcast.7, f32[1024,128]{1,0:T(8,128)} %bitcast.8), custom_call_target="tpu_custom_call" | custom-call | tf_op jit(solution)/shard_map/factors/pallas_call | solution.py:636
  55.6 4.8 %finish.1 = (f32[2048,1024]{1,0:T(8,128)}, bf16[2048,1024]{1,0:T(8,128)(2,1)}, f32[1024,128]{1,0:T(8,128)}) custom-call(f32[2048,1024]{1,0:T(8,128)S(1)} %get-tuple-element.9.mixed_ref, bf16[2048,256]{1,0:T(8,128)(2,1)S(1)} %get-tuple-element.10.pair_ref, f32[1024,128]{1,0:T(8,128)S(1)} %get-tuple-element.11.following_ref), custom_call_target="tpu_custom_call" | custom-call | tf_op jit(solution)/shard_map/finish/pallas_call | solution.py:683

commit v7 on v6

--- a/solution.py
+++ b/solution.py
@@ -204,10 +204,11 @@
         return place(half, chip(chips - 1 - i)[0])
 
     prior_copy = pltpu.make_async_copy(prior_ref, prior_vmem, prior_sem)
-    prior_copy.start()
     for slot in range(min(AHEAD, loads)):
         for copy in load(slot, spot(slot)):
             copy.start()
+        if slot == 0:
+            prior_copy.start()
 
     barrier = pltpu.get_barrier_semaphore()
     for k in range(1, plane):
@@ -345,6 +346,16 @@
         gram_across(0)
     with jax.named_scope("p6_gram2"):
         gram_spread(0)
+    def refine(half):
+        block = rows // STEPS
+        for i in range(STEPS // cores):
+            at = pl.ds(pl.multiple_of(half * (rows // cores) + i * block, 8), block)
+            high, middle_part, low = split3(whole[at, :])
+            fine[0, at, :rank] = high
+            fine[0, at, rank:] = middle_part
+            fine[1, at, :rank] = high
+            fine[1, at, rank:] = low
+
     with jax.named_scope("p7_agwait"):
         if chips > 1:
             bulk(1).wait_send()
@@ -354,6 +365,7 @@
             remote(left.at[at], left.at[at], once.at[0], once.at[0], partner).wait_send()
             half_copy = remote(whole.at[at], whole.at[at], once.at[5], once.at[6], partner)
             half_copy.start()
+            refine(core)
     with jax.named_scope("p8_gram3"):
         gram = gram_whole(0)
     parts = 2 if rank % 16 == 0 else 1
@@ -413,15 +425,11 @@
                         step(u, True) if step is far else step(u)
 
     def basis_half(r, w):
+        if r == 0:
+            refine(cores - 1 - core)
         for i in range(STEPS):
             block = rows // STEPS
             at = slice(i * block, (i + 1) * block)
-            if r == 0:
-                high, middle_part, low = split3(whole[at, :])
-                fine[0, at, :rank] = high
-                fine[0, at, rank:] = middle_part
-                fine[1, at, :rank] = high
-                fine[1, at, rank:] = low
             value = value_of(w, fine[0, at, :], fine[1, at, :])
             high, low = split(value)
             turned[r, :tall, at] = high

time: 60.7 us -> 60.8 us (level)
  no operation moved by 1% of the time
where the time goes in v7:
time: 60.8 us; the launch traced here: 60.7 us
  Pallas kernels  59.9 us (99%)
  between operations  0.8 us (1%)
    pallas_call x1, Pallas kernels, shards(): pl.pallas_call(functools.partial(factors, shape), out_shape=[pltpu.VMEM((...  55 us
    pallas_call x1, Pallas kernels, shards(): pl.pallas_call(functools.partial(finish, scale), out_shape=[jax.ShapeDtyp...  4.84 us

profile of v7, /device:TPU:0, one launch (start us, length us, event | category | flops | bytes accessed | tf_op | source)
XLA Modules:
  0.0 60.7 jit_solution(11986055574809011394)
XLA Ops:
  0.6 55.0 %factors.1 = (f32[2048,1024]{1,0:T(8,128)S(1)}, bf16[2048,256]{1,0:T(8,128)(2,1)S(1)}, f32[1024,128]{1,0:T(8,128)S(1)}) custom-call(f32[2048,1024]{1,0:T(8,128)} %bitcast.6, bf16[2048,1024]{1,0:T(8,128)(2,1)} %bitcast.7, f32[1024,128]{1,0:T(8,128)} %bitcast.8), custom_call_target="tpu_custom_call" | custom-call | tf_op jit(solution)/shard_map/factors/pallas_call | solution.py:644
  55.7 4.8 %finish.1 = (f32[2048,1024]{1,0:T(8,128)}, bf16[2048,1024]{1,0:T(8,128)(2,1)}, f32[1024,128]{1,0:T(8,128)}) custom-call(f32[2048,1024]{1,0:T(8,128)S(1)} %get-tuple-element.9.mixed_ref, bf16[2048,256]{1,0:T(8,128)(2,1)S(1)} %get-tuple-element.10.pair_ref, f32[1024,128]{1,0:T(8,128)S(1)} %get-tuple-element.11.following_ref), custom_call_target="tpu_custom_call" | custom-call | tf_op jit(solution)/shard_map/finish/pallas_call | solution.py:691

commit v8 on v6

--- a/solution.py
+++ b/solution.py
@@ -204,10 +204,11 @@
         return place(half, chip(chips - 1 - i)[0])
 
     prior_copy = pltpu.make_async_copy(prior_ref, prior_vmem, prior_sem)
-    prior_copy.start()
     for slot in range(min(AHEAD, loads)):
         for copy in load(slot, spot(slot)):
             copy.start()
+        if slot == 0:
+            prior_copy.start()
 
     barrier = pltpu.get_barrier_semaphore()
     for k in range(1, plane):

time: 60.7 us -> 60.7 us (level)
  no operation moved by 1% of the time
where the time goes in v8:
time: 60.7 us; the launch traced here: 60.6 us
  Pallas kernels  59.8 us (99%)
  between operations  0.8 us (1%)
    pallas_call x1, Pallas kernels, shards(): pl.pallas_call(functools.partial(factors, shape), out_shape=[pltpu.VMEM((...  54.9 us
    pallas_call x1, Pallas kernels, shards(): pl.pallas_call(functools.partial(finish, scale), out_shape=[jax.ShapeDtyp...  4.84 us

profile of v8, /device:TPU:0, one launch (start us, length us, event | category | flops | bytes accessed | tf_op | source)
XLA Modules:
  0.0 60.6 jit_solution(5008513262978359397)
XLA Ops:
  0.6 54.9 %factors.1 = (f32[2048,1024]{1,0:T(8,128)S(1)}, bf16[2048,256]{1,0:T(8,128)(2,1)S(1)}, f32[1024,128]{1,0:T(8,128)S(1)}) custom-call(f32[2048,1024]{1,0:T(8,128)} %bitcast.6, bf16[2048,1024]{1,0:T(8,128)(2,1)} %bitcast.7, f32[1024,128]{1,0:T(8,128)} %bitcast.8), custom_call_target="tpu_custom_call" | custom-call | tf_op jit(solution)/shard_map/factors/pallas_call | solution.py:637
  55.6 4.8 %finish.1 = (f32[2048,1024]{1,0:T(8,128)}, bf16[2048,1024]{1,0:T(8,128)(2,1)}, f32[1024,128]{1,0:T(8,128)}) custom-call(f32[2048,1024]{1,0:T(8,128)S(1)} %get-tuple-element.9.mixed_ref, bf16[2048,256]{1,0:T(8,128)(2,1)S(1)} %get-tuple-element.10.pair_ref, f32[1024,128]{1,0:T(8,128)S(1)} %get-tuple-element.11.following_ref), custom_call_target="tpu_custom_call" | custom-call | tf_op jit(solution)/shard_map/finish/pallas_call | solution.py:684
